TPU v7x, 128 devices: a whole 4x4x4 slice. The times are simulated.
128 devices in a mesh: depth: 8 (over x, core), rows: 16 (over z, y).
Axes of the slice: x: 4, y: 4, z: 4, core: 2. Of those that a mesh axis runs over, the one named last changes fastest.
Arguments:
- volume: bfloat16 [4, 128, 512, 4096], P(None, 'depth', 'rows')
- shear_rows: int32 [128], P('depth'), may hold values from -8 to 8, as said below
- shear_cols: int32 [128], P('depth'), may hold values from -8 to 8, as said below
- warp_cols: int32 [512], replicated, may hold values from -8 to 8, as said below
- warp_rows: int32 [4096], P('depth'), may hold values from -8 to 8, as said below
Outputs:
- final_image: float32 [4, 512, 4096], P(None, 'rows', 'depth')
Inputs may be any that keep to these rules, and one draw needn't show every extreme that they name: `shear_rows`: both -8 and 8 occur. `shear_cols`: both -8 and 8 occur. `warp_cols`: both -8 and 8 occur. `warp_rows`: both -8 and 8 occur.
All inputs are finite; a program needn't handle non-finite values.
Results may differ from a plain program's by a relative error of at most 0.0017.
Values may be sent and summed in bfloat16 or wider, within the bound.
No kernel may reach another device: no remote copies, remote signals or barrier semaphores. Data moves between devices by JAX's collectives and lax.ppermute only.
A program may use at most 192 MiB of HBM per device.

v0:
```python
import jax
import jax.numpy as jnp
from jax import lax
from jax.sharding import PartitionSpec as P

SHIFT = 8


def extended_2(block, sides, width):
    for axis, dim in sides:
        count = lax.axis_size(axis)
        forward = [(i, i + 1) for i in range(count - 1)]
        backward = [(target, source) for source, target in forward]
        low = lax.ppermute(
            lax.slice_in_dim(block, block.shape[dim] - width, None, axis=dim), axis, forward
        )
        high = lax.ppermute(lax.slice_in_dim(block, 0, width, axis=dim), axis, backward)
        block = jnp.concatenate([low, block, high], axis=dim)
    return block


def swapped(value, axis, distance):
    mask = 2**distance
    pairs = [(source, source ^ mask) for source in range(lax.axis_size(axis))]
    return lax.ppermute(value, axis, pairs)


def weight_of(offset):
    return jnp.where(offset == 0, 0.5, jnp.where(jnp.abs(offset) == 1, 0.25, 0.0)).astype(
        jnp.float32
    )


def over_front(front_part, back_part):
    return front_part + (1.0 - front_part[3:4]) * back_part


def premultiply(slab):
    opacity = slab[3:4]
    return jnp.concatenate([slab[:3] * opacity, opacity], 0)


def shear_slice(extended, row_shift, col_shift, band_rows, band_cols, rim_width):
    band_sum = jnp.zeros((4, band_rows, band_cols + 2 * rim_width), jnp.float32)
    for offset, factor in ((-1, 0.25), (0, 0.5), (1, 0.25)):
        start = rim_width + row_shift + offset
        band_sum = band_sum + factor * lax.dynamic_slice_in_dim(extended, start, band_rows, 1)
    sheared = jnp.zeros((4, band_rows, band_cols), jnp.float32)
    for offset, factor in ((-1, 0.25), (0, 0.5), (1, 0.25)):
        start = rim_width + col_shift + offset
        sheared = sheared + factor * lax.dynamic_slice_in_dim(band_sum, start, band_cols, 2)
    return sheared


def shift_columns(picture, shifts, band_cols, rim_width):
    result = jnp.zeros((4, picture.shape[1], band_cols), jnp.float32)
    for offset in range(-rim_width, rim_width + 1):
        kernel_col = weight_of(offset - shifts)[None, :, None]
        result = (
            result + kernel_col * picture[:, :, rim_width + offset : rim_width + offset + band_cols]
        )
    return result


def shift_rows(picture, shifts, band_rows, rim_width):
    result = jnp.zeros((4, band_rows, picture.shape[2]), jnp.float32)
    for offset in range(-rim_width, rim_width + 1):
        kernel_row = weight_of(offset - shifts)[None, None, :]
        result = (
            result + kernel_row * picture[:, rim_width + offset : rim_width + offset + band_rows, :]
        )
    return result


def per_device(volume, shear_rows, shear_cols, warp_cols, warp_rows):
    rim_width = SHIFT + 1
    slab_count = volume.shape[1]
    band_rows = volume.shape[2]
    band_cols = volume.shape[3]
    extended_volume = extended_2(volume, (("rows", 2),), rim_width)

    def add_slice(index, accumulated):
        slice_now = lax.dynamic_index_in_dim(extended_volume, index, 1, keepdims=False)
        extended = jnp.pad(
            premultiply(slice_now.astype(jnp.float32)), ((0, 0), (0, 0), (rim_width, rim_width))
        )
        sheared = shear_slice(
            extended, shear_rows[index], shear_cols[index], band_rows, band_cols, rim_width
        )
        return over_front(accumulated, sheared)

    partial_image = lax.fori_loop(
        0, slab_count, add_slice, jnp.zeros((4, band_rows, band_cols), jnp.float32)
    )
    depth_count = lax.axis_size("depth")
    tile_cols = band_cols // depth_count
    bit_count = depth_count.bit_length() - 1
    position = lax.axis_index("depth")
    pieces = partial_image.reshape((4, band_rows) + (2,) * bit_count + (tile_cols,))
    for bit in range(bit_count):
        bit_axis = 2 + bit_count - 1 - bit
        low_half = lax.slice_in_dim(pieces, 0, 1, axis=bit_axis)
        high_half = lax.slice_in_dim(pieces, 1, 2, axis=bit_axis)
        upper_side = jnp.right_shift(position, bit) % 2 == 1
        kept_half = jnp.where(upper_side, high_half, low_half)
        sent_half = jnp.where(upper_side, low_half, high_half)
        received = swapped(sent_half.astype(jnp.bfloat16), "depth", bit).astype(sent_half.dtype)
        pieces = jnp.where(
            upper_side, over_front(received, kept_half), over_front(kept_half, received)
        )
    tile_image = pieces.reshape((4, band_rows, tile_cols))
    row_start = lax.axis_index("rows") * band_rows
    column_tile = extended_2(tile_image, (("depth", 2),), rim_width)
    row_shifts = lax.dynamic_slice_in_dim(warp_cols, row_start, band_rows, 0)
    across = shift_columns(column_tile, row_shifts, tile_cols, rim_width)
    row_tile = extended_2(across, (("rows", 1),), rim_width)
    final_image = shift_rows(row_tile, warp_rows, band_rows, rim_width)
    return final_image


def solution(mesh):
    return jax.shard_map(
        per_device,
        mesh=mesh,
        in_specs=(P(None, "depth", "rows", None), P("depth"), P("depth"), P(), P("depth")),
        out_specs=P(None, "rows", "depth"),
        check_vma=False,
    )
```

profile of v0, /device:TPU:24, one launch (start us, length us, event | category | flops | bytes accessed | tf_op | source)
XLA Modules:
  0.0 516.2 jit_solution(13992808587979035224)
XLA Ops:
  0.0 7.2 %fusion.110 = (bf16[4,16,9,4096]{3,2,1,0:T(8,128)(2,1)S(1)}, bf16[4,16,9,4096]{3,2,1,0:T(8,128)(2,1)S(1)}) fusion(bf16[4,16,32,4096]{3,2,1,0:T(8,128)(2,1)} %param.7), kind=kLoop, calls=%fused_computation.289 | loop fusion | bytes 18874368 | tf_op jit(solution)/shard_map/slice | solution.py:15
  7.3 5.0 copy.19
  15.7 5.0 copy.20
  24.1 93.9 %collective-permute-done = bf16[4,16,9,4096]{3,1,2,0:T(8,128)(2,1)} collective-permute-done((bf16[4,16,9,4096]{3,1,2,0:T(8,128)(2,1)}, bf16[4,16,9,4096]{3,1,2,0:T(8,128)(2,1)}, u32[]{:S(2)}, u32[]{:S(2)}) %collective-permute-start) | collective-permute-done | bytes 4718624 | tf_op jit(solution)/shard_map/ppermute | solution.py:14
  118.0 8.9 %copy.8 = bf16[4,16,9,4096]{3,2,1,0:T(8,128)(2,1)} copy(bf16[4,16,9,4096]{3,1,2,0:T(8,128)(2,1)} %collective-permute-done) | data formatting | bytes 9437184 | tf_op jit(solution)/shard_map/ppermute | solution.py:14
  128.4 8.8 %copy.9 = bf16[4,16,9,4096]{3,2,1,0:T(8,128)(2,1)} copy(bf16[4,16,9,4096]{3,1,2,0:T(8,128)(2,1)} %collective-permute-done.1) | data formatting | bytes 9437184 | tf_op jit(solution)/shard_map/ppermute | solution.py:17
  137.2 21.8 %pad_maximum_fusion = bf16[4,16,50,4096]{3,2,1,0:T(8,128)(2,1)} fusion(bf16[4,16,9,4096]{3,2,1,0:T(8,128)(2,1)} %copy.9, bf16[4,16,32,4096]{3,2,1,0:T(8,128)(2,1)} %param.7, bf16[4,16,9,4096]{3,2,1,0:T(8,128)(2,1)} %copy.8), kind=kLoop, calls=%fused_computation.14 | loop fusion | flops 78643200 | bytes 52428800 | tf_op jit(solution)/shard_map/concatenate | solution.py:18
  159.0 296.5 %while.19 = (s32[]{:T(128)}, f32[4,32,4096]{2,1,0:T(8,128)}, bf16[4,16,50,4096]{3,2,1,0:T(8,128)(2,1)}, s32[16]{0:T(128)S(1)}, s32[16]{0:T(128)S(1)}, /*index=5*...) while((s32[]{:T(128)}, f32[4,32,4096]{2,1,0:T(8,128)}, ...), condition=%wide.region_1.2_spmd.clone, body=%wide.region_0.1_spmd.clone.sunk | while | flops 13853051 | bytes 44354072 | solution.py:92
  188.7 4.6 multiply_add_fusion.5
  207.4 4.6 multiply_add_fusion.5
  226.1 4.6 multiply_add_fusion.5
  244.8 4.6 multiply_add_fusion.5
  263.6 4.6 multiply_add_fusion.5
  282.3 4.6 multiply_add_fusion.5
  301.1 4.6 multiply_add_fusion.5
  319.8 4.6 multiply_add_fusion.5
  338.5 4.6 multiply_add_fusion.5
  357.2 4.6 multiply_add_fusion.5
  375.9 4.6 multiply_add_fusion.5
  413.4 4.6 multiply_add_fusion.5
  432.1 4.6 multiply_add_fusion.5
  469.7 11.7 %collective-permute-done.3 = bf16[4,32,2,1,1,512]{5,4,3,2,1,0:T(2,128)(2,1)S(1)} collective-permute-done((bf16[4,32,2,1,1,512]{5,4,3,2,1,0:T(2,128)(2,1)S(1)}, bf16[4,32,2,1,1,512]{5,4,3,2,1,0:T(2,128)(2,1)S(1)}, u32[]{:S(2)}, u32[]{:S(2)}) %collective-permute-start.3) | collective-permute-done | bytes 262176 | tf_op jit(solution)/shard_map/ppermute | solution.py:25
  486.9 5.8 %collective-permute-done.4 = bf16[4,32,1,1,1,512]{5,4,3,2,1,0:T(2,128)(2,1)S(1)} collective-permute-done((bf16[4,32,1,1,1,512]{5,4,3,2,1,0:T(2,128)(2,1)S(1)}, bf16[4,32,1,1,1,512]{5,4,3,2,1,0:T(2,128)(2,1)S(1)}, u32[]{:S(2)}, u32[]{:S(2)}) %collective-permute-start.4) | collective-permute-done | bytes 131104 | tf_op jit(solution)/shard_map/ppermute | solution.py:25
  508.5 6.3 %collective-permute-done.8 = f32[4,9,512]{2,1,0:T(8,128)S(1)} collective-permute-done((f32[4,9,512]{2,1,0:T(8,128)S(1)}, f32[4,9,512]{2,1,0:T(8,128)S(1)}, u32[]{:S(2)}, u32[]{:S(2)}) %collective-permute-start.8) | collective-permute-done | bytes 73760 | tf_op jit(solution)/shard_map/ppermute | solution.py:17
  (202 shorter events, 169.6 us)
Async XLA Ops:
  12.3 105.7 %collective-permute-start = (bf16[4,16,9,4096]{3,1,2,0:T(8,128)(2,1)}, bf16[4,16,9,4096]{3,1,2,0:T(8,128)(2,1)}, u32[]{:S(2)}, u32[]{:S(2)}) collective-permute-start(bf16[4,16,9,4096]{3,1,2,0:T(8,128)(2,1)} %copy.19), channel_id=1, source_target_pairs={{0,1},{1,2},{2,3},{3,4},{4,5},{5,6},{6,7},{7,8},{8,9},{9,10},{10,1... | collective-permute-start | bytes 14155784 | tf_op jit(solution)/shard_map/ppermute | solution.py:14
  20.8 107.6 %collective-permute-start.1 = (bf16[4,16,9,4096]{3,1,2,0:T(8,128)(2,1)}, bf16[4,16,9,4096]{3,1,2,0:T(8,128)(2,1)}, u32[]{:S(2)}, u32[]{:S(2)}) collective-permute-start(bf16[4,16,9,4096]{3,1,2,0:T(8,128)(2,1)} %copy.20), channel_id=1, source_target_pairs={{1,0},{2,1},{3,2},{4,3},{5,4},{6,5},{7,6},{8,7},{9,8},{10,9},{11,1... | collective-permute-start | bytes 14155784 | tf_op jit(solution)/shard_map/ppermute | solution.py:17
  137.2 21.8 %copy-start.1 = (s32[16]{0:T(128)S(1)}, s32[16]{0:T(128)}, u32[]{:S(2)}) copy-start(s32[16]{0:T(128)} %param.8) | copy-start | bytes 196
  137.2 21.8 %copy-start.2 = (s32[16]{0:T(128)S(1)}, s32[16]{0:T(128)}, u32[]{:S(2)}) copy-start(s32[16]{0:T(128)} %param.9) | copy-start | bytes 196
  460.4 2.0 collective-permute-start.2
  467.3 14.1 %collective-permute-start.3 = (bf16[4,32,2,1,1,512]{5,4,3,2,1,0:T(2,128)(2,1)S(1)}, bf16[4,32,2,1,1,512]{5,4,3,2,1,0:T(2,128)(2,1)S(1)}, u32[]{:S(2)}, u32[]{:S(2)}) collective-permute-start(bf16[4,32,2,1,1,512]{5,4,3,2,1,0:T(2,128)(2,1)S(1)} %fusion.4), channel_id=1, source_target_pairs={{0,32},{16,48},{32,0},{48,16},{64,96},{80,112},{96,64},{112,80},{1... | collective-permute-start | bytes 786440 | tf_op jit(solution)/shard_map/ppermute | solution.py:25
  483.1 24.7 %copy-start = (s32[512]{0:T(512)S(1)}, s32[512]{0:T(512)}, u32[]{:S(2)}) copy-start(s32[512]{0:T(512)} %param.11) | copy-start | bytes 6148
  483.6 9.1 %collective-permute-start.4 = (bf16[4,32,1,1,1,512]{5,4,3,2,1,0:T(2,128)(2,1)S(1)}, bf16[4,32,1,1,1,512]{5,4,3,2,1,0:T(2,128)(2,1)S(1)}, u32[]{:S(2)}, u32[]{:S(2)}) collective-permute-start(bf16[4,32,1,1,1,512]{5,4,3,2,1,0:T(2,128)(2,1)S(1)} %fusion.55), channel_id=1, source_target_pairs={{0,64},{16,80},{32,96},{48,112},{64,0},{80,16},{96,32},{112,48},{1... | collective-permute-start | bytes 393224 | tf_op jit(solution)/shard_map/ppermute | solution.py:25
  493.7 2.6 collective-permute-start.5
  495.0 4.9 collective-permute-start.6
  501.6 6.9 %collective-permute-start.7 = (f32[4,9,512]{2,1,0:T(8,128)S(1)}, f32[4,9,512]{2,1,0:T(8,128)S(1)}, u32[]{:S(2)}, u32[]{:S(2)}) collective-permute-start(f32[4,9,512]{2,1,0:T(8,128)S(1)} %get-tuple-element.244), channel_id=1, source_target_pairs={{0,1},{1,2},{2,3},{3,4},{4,5},{5,6},{6,7},{7,8},{8,9},{9,10},{10,1... | collective-permute-start | bytes 221192 | tf_op jit(solution)/shard_map/ppermute | solution.py:14
  505.8 9.0 %collective-permute-start.8 = (f32[4,9,512]{2,1,0:T(8,128)S(1)}, f32[4,9,512]{2,1,0:T(8,128)S(1)}, u32[]{:S(2)}, u32[]{:S(2)}) collective-permute-start(f32[4,9,512]{2,1,0:T(8,128)S(1)} %get-tuple-element.245), channel_id=1, source_target_pairs={{1,0},{2,1},{3,2},{4,3},{5,4},{6,5},{7,6},{8,7},{9,8},{10,9},{11,1... | collective-permute-start | bytes 221192 | tf_op jit(solution)/shard_map/ppermute | solution.py:17
where the time goes:
time: 522 us; the launch traced here: 516 us
  other arithmetic  201 us (39%)
  waiting for transfers between devices  124 us (24%)
  loops' own time  111 us (21%)
  local copies, waits for them, and re-layouts  60.5 us (12%)
  starting transfers between devices  19.6 us (4%)
    another operation x1, loops' own time, per_device(): lax.fori_loop(0, slab_count, add_slice, jnp.zeros((4, band_rows, band_col...  111 us
    ppermute x3, waiting for transfers between devices, extended_2(): lax.ppermute(lax.slice_in_dim(block, block.shape[dim] - width, None, axis...  94.6 us
    add x16, other arithmetic, over_front(): return front_part + (1.0 - front_part[3:4]) * back_part  72.7 us
    convert_element_type x16, other arithmetic, add_slice(): slice_now.astype(jnp.float32)  30.7 us
    while x16, other arithmetic  26.3 us
    concatenate x1, other arithmetic, extended_2(): block = jnp.concatenate([low, block, high], axis=dim)  21.8 us
    ppermute x3, waiting for transfers between devices, swapped(): return lax.ppermute(value, axis, pairs)  17.9 us
    concatenate x16, other arithmetic, premultiply(): return jnp.concatenate([slab[:3] * opacity, opacity], 0)  16.6 us
  transfers between devices with their start and end apart: 9, of which 8 were waited for; matrix products, arithmetic and copies ran while one was open for 3% of the time, Pallas kernels for 0%

commit v1 on v0

v1 whole, which is shorter than its diff:
```python
import functools

import jax
import jax.numpy as jnp
from jax import lax
from jax.experimental import pallas as pl
from jax.experimental.pallas import tpu as pltpu
from jax.sharding import PartitionSpec as P

SHIFT = 8
RIM = SHIFT + 1
BLOCK = 256
EDGE = 128
VMEM_LIMIT = 60 * 1024 * 1024


def rows_from_high(shift):
    return jnp.maximum(shift + 1, 0)


def rows_from_low(shift):
    return jnp.maximum(1 - shift, 0)


def pack_kernel(shear_rows, top_ref, bottom_ref, up_ref, down_ref, up_rows, down_rows, used):
    index = pl.program_id(0)
    slots = up_ref.shape[0] * 8
    tiles = up_ref.shape[3] // 128

    @pl.when(index == 0)
    def _():
        used[0] = 0
        used[1] = 0

    def scatter(source, target, row):
        def body(tile, carry):
            lane = pl.multiple_of(tile * 128, 128)
            for channel in range(4):
                target[tile, channel, pl.ds(row, 16), :] = source[
                    channel, 0, :, pl.ds(lane, 128)
                ].astype(jnp.float32)
            return carry

        lax.fori_loop(0, tiles, body, 0)

    shift = shear_rows[index]
    up_count = rows_from_high(shift)
    down_count = rows_from_low(shift)

    @pl.when(up_count > 0)
    def _():
        scatter(top_ref, up_rows, used[0])

    @pl.when(down_count > 0)
    def _():
        scatter(bottom_ref, down_rows, slots - used[1])

    used[0] = used[0] + up_count
    used[1] = used[1] + down_count

    @pl.when(index == pl.num_programs(0) - 1)
    def _():
        def flush(group, carry):
            row = pl.multiple_of(group * 8, 8)
            for tile in range(tiles):
                lanes = slice(tile * 128, tile * 128 + 128)
                for channel in range(4):
                    up_ref[group, channel, :, lanes] = up_rows[
                        tile, channel, pl.ds(row, 8), :
                    ].astype(jnp.bfloat16)
                    down_ref[group, channel, :, lanes] = down_rows[
                        tile, channel, pl.ds(pl.multiple_of(row + 16, 8), 8), :
                    ].astype(jnp.bfloat16)
            return carry

        lax.fori_loop(0, up_ref.shape[0], flush, 0)


def pack_halo(volume, shear_rows):
    _, slices, band_rows, columns = volume.shape
    groups = -(-RIM * slices // 8)
    last = band_rows // 16 - 1
    packed = jax.ShapeDtypeStruct((groups, 4, 8, columns), jnp.bfloat16)
    whole = pl.BlockSpec((groups, 4, 8, columns), lambda i, s: (0, 0, 0, 0), pipeline_mode=pl.Buffered(1))
    return pl.pallas_call(
        pack_kernel,
        out_shape=(packed, packed),
        grid_spec=pltpu.PrefetchScalarGridSpec(
            num_scalar_prefetch=1,
            grid=(slices,),
            in_specs=[
                pl.BlockSpec((4, 1, 16, columns), lambda i, s: (0, i, 0, 0)),
                pl.BlockSpec((4, 1, 16, columns), lambda i, s: (0, i, last, 0)),
            ],
            out_specs=[whole, whole],
            scratch_shapes=[
                pltpu.VMEM((columns // 128, 4, groups * 8 + 16, 128), jnp.float32),
                pltpu.VMEM((columns // 128, 4, groups * 8 + 16, 128), jnp.float32),
                pltpu.SMEM((2,), jnp.int32),
            ],
        ),
        compiler_params=pltpu.CompilerParams(vmem_limit_bytes=VMEM_LIMIT),
    )(shear_rows, volume, volume)


def shear_kernel(
    shear_rows, shear_cols, volume_ref, low_ref, high_ref, image_ref,
    inner, rim_low, rim_high, weights, filtered, total, used,
):
    index = pl.program_id(0)
    band_rows = volume_ref.shape[2]
    columns = volume_ref.shape[3]
    blocks = columns // BLOCK
    groups = low_ref.shape[0]
    row_shift = shear_rows[index]
    col_shift = shear_cols[index]

    @pl.when(index == 0)
    def _():
        used[0] = 0
        used[1] = 0
        for part in (inner, rim_low, rim_high):
            part[:, 0:EDGE] = jnp.zeros((part.shape[0], EDGE), jnp.bfloat16)
            part[:, EDGE + columns :] = jnp.zeros((part.shape[0], EDGE), jnp.bfloat16)

        def clear(block, carry):
            start = pl.multiple_of(block * BLOCK, BLOCK)
            for channel in range(4):
                total[channel, :, pl.ds(start, BLOCK)] = jnp.full(
                    (band_rows, BLOCK), 0.0 if channel < 3 else 1.0, jnp.float32
                )
            return carry

        lax.fori_loop(0, blocks, clear, 0)

    high_count = rows_from_high(row_shift)
    low_count = rows_from_low(row_shift)
    high_start = used[0]
    low_start = groups * 8 - used[1] - low_count
    used[0] = used[0] + high_count
    used[1] = used[1] + low_count
    high_group = jnp.minimum(high_start // 8, groups - 2)
    low_group = jnp.minimum(low_start // 8, groups - 2)
    high_row = 16 + band_rows - (high_start - high_group * 8)
    low_row = 16 - low_count - (low_start - low_group * 8)

    source = lax.broadcasted_iota(jnp.int32, (2 * BLOCK, BLOCK), 0)
    target = lax.broadcasted_iota(jnp.int32, (2 * BLOCK, BLOCK), 1)
    distance = jnp.abs(source - target - EDGE - col_shift)
    weights[...] = jnp.where(
        distance == 0, 0.125, jnp.where(distance == 1, 0.0625, 0.0)
    ).astype(jnp.bfloat16)

    def premultiply(block, carry):
        start = pl.multiple_of(block * BLOCK, BLOCK)
        place = pl.multiple_of(start + EDGE, EDGE)
        opacity = volume_ref[3, 0, :, pl.ds(start, BLOCK)].astype(jnp.float32)
        for channel in range(4):
            value = volume_ref[channel, 0, :, pl.ds(start, BLOCK)].astype(jnp.float32)
            if channel < 3:
                value = value * opacity
            inner[pl.ds(channel * band_rows, band_rows), pl.ds(place, BLOCK)] = value.astype(
                jnp.bfloat16
            )
        return carry

    lax.fori_loop(0, blocks, premultiply, 0)

    def premultiply_rim(packed, group, rim):
        def body(block, carry):
            start = pl.multiple_of(block * BLOCK, BLOCK)
            place = pl.multiple_of(start + EDGE, EDGE)

            def rows_of(channel):
                return jnp.concatenate(
                    [packed[group + half, channel, :, pl.ds(start, BLOCK)].astype(jnp.float32) for half in range(2)], 0
                )

            opacity = rows_of(3)
            for channel in range(4):
                value = rows_of(channel) * opacity if channel < 3 else opacity
                rim[pl.ds(channel * 16, 16), pl.ds(place, BLOCK)] = value.astype(jnp.bfloat16)
            return carry

        lax.fori_loop(0, blocks, body, 0)

    @pl.when(low_count > 0)
    def _():
        premultiply_rim(low_ref, low_group, rim_low)

    @pl.when(high_count > 0)
    def _():
        premultiply_rim(high_ref, high_group, rim_high)

    def filter_columns(part, start):
        return jnp.dot(
            part[:, pl.ds(start, 2 * BLOCK)], weights[...], preferred_element_type=jnp.float32
        )

    def composite(block, carry):
        start = pl.multiple_of(block * BLOCK, BLOCK)

        @pl.when(low_count > 0)
        def _():
            rows = filter_columns(rim_low, start)
            for channel in range(4):
                for tile in range(BLOCK // 128):
                    filtered[tile, channel, pl.ds(low_row, 16), :] = rows[
                        channel * 16 : channel * 16 + 16, tile * 128 : tile * 128 + 128
                    ]

        @pl.when(high_count > 0)
        def _():
            rows = filter_columns(rim_high, start)
            for channel in range(4):
                for tile in range(BLOCK // 128):
                    filtered[tile, channel, pl.ds(high_row, 16), :] = rows[
                        channel * 16 : channel * 16 + 16, tile * 128 : tile * 128 + 128
                    ]

        rows = filter_columns(inner, start)
        for channel in range(4):
            for tile in range(BLOCK // 128):
                filtered[tile, channel, 16 : 16 + band_rows, :] = rows[
                    channel * band_rows : (channel + 1) * band_rows, tile * 128 : tile * 128 + 128
                ]
        for tile in range(BLOCK // 128):
            lanes = pl.ds(pl.multiple_of(start + tile * 128, 128), 128)

            def sheared(channel):
                first, middle, last = (
                    filtered[tile, channel, pl.ds(16 + row_shift + offset, band_rows), :]
                    for offset in (-1, 0, 1)
                )
                return first + last + (middle + middle)

            passed = total[3, :, lanes]
            for channel in range(3):
                total[channel, :, lanes] = total[channel, :, lanes] + passed * sheared(channel)
            total[3, :, lanes] = passed - passed * sheared(3)
        return carry

    lax.fori_loop(0, blocks, composite, 0)

    @pl.when(index == pl.num_programs(0) - 1)
    def _():
        tiles = image_ref.shape[0]
        width = columns // tiles
        lane = lax.broadcasted_iota(jnp.int32, (band_rows, EDGE), 1)
        zero = jnp.zeros((band_rows, EDGE), jnp.float32)
        for channel in range(4):

            def value(start, size):
                part = total[channel, :, pl.ds(start, size)]
                return part if channel < 3 else 1.0 - part

            for tile in range(tiles):
                first = tile * width
                image_ref[tile, channel, :, 0:width] = value(first, width).astype(jnp.bfloat16)
                before = value(first - EDGE, EDGE) if tile > 0 else zero
                after = value(first + width, EDGE) if tile < tiles - 1 else zero
                image_ref[tile, channel, :, width:] = jnp.where(
                    lane < EDGE // 2, after, before
                ).astype(jnp.bfloat16)


def shear_slab(volume, shear_rows, shear_cols, low, high, tiles):
    _, slices, band_rows, columns = volume.shape
    groups = low.shape[0]
    whole = pl.BlockSpec((groups, 4, 8, columns), lambda i, a, b: (0, 0, 0, 0), pipeline_mode=pl.Buffered(1))
    image = (tiles, 4, band_rows, columns // tiles + EDGE)
    return pl.pallas_call(
        shear_kernel,
        out_shape=jax.ShapeDtypeStruct(image, jnp.bfloat16),
        grid_spec=pltpu.PrefetchScalarGridSpec(
            num_scalar_prefetch=2,
            grid=(slices,),
            in_specs=[
                pl.BlockSpec((4, 1, band_rows, columns), lambda i, a, b: (0, i, 0, 0)),
                whole,
                whole,
            ],
            out_specs=pl.BlockSpec(image, lambda i, a, b: (0, 0, 0, 0), pipeline_mode=pl.Buffered(1)),
            scratch_shapes=[
                pltpu.VMEM((4 * band_rows, columns + 2 * EDGE), jnp.bfloat16),
                pltpu.VMEM((64, columns + 2 * EDGE), jnp.bfloat16),
                pltpu.VMEM((64, columns + 2 * EDGE), jnp.bfloat16),
                pltpu.VMEM((2 * BLOCK, BLOCK), jnp.bfloat16),
                pltpu.VMEM((BLOCK // 128, 4, band_rows + 32, 128), jnp.float32),
                pltpu.VMEM((4, band_rows, columns), jnp.float32),
                pltpu.SMEM((2,), jnp.int32),
            ],
        ),
        compiler_params=pltpu.CompilerParams(vmem_limit_bytes=VMEM_LIMIT),
    )(shear_rows, shear_cols, volume, low, high)


def weight_of(offset):
    return jnp.where(offset == 0, 0.5, jnp.where(jnp.abs(offset) == 1, 0.25, 0.0))


def across_kernel(pieces_ref, shifts_ref, across_ref, top_ref, bottom_ref):
    tiles, _, band_rows, padded = pieces_ref.shape
    width = across_ref.shape[2]
    for row in range(0, band_rows, 8):
        rows = slice(row, row + 8)
        totals = [None] * 4
        passed = None
        for tile in range(tiles):
            parts = [pieces_ref[tile, channel, rows, :].astype(jnp.float32) for channel in range(4)]
            if tile == 0:
                totals = parts[:3]
                passed = 1.0 - parts[3]
            else:
                totals = [total + passed * part for total, part in zip(totals, parts[:3])]
                passed = passed - passed * parts[3]
        totals = totals[:3] + [1.0 - passed]
        shifts = jnp.broadcast_to(shifts_ref[rows, :], (8, width))
        results = [jnp.zeros((8, width), jnp.float32)] * 4
        for offset in range(-RIM, RIM + 1):
            factor = weight_of(offset - shifts)
            for channel in range(4):
                moved = pltpu.roll(totals[channel], (-offset) % padded, 1)[:, :width]
                results[channel] = results[channel] + factor * moved
        for channel in range(4):
            across_ref[channel, rows, :] = results[channel]
    for channel in range(4):
        top_ref[channel * RIM : (channel + 1) * RIM, :] = across_ref[channel, 0:RIM, :]
        bottom_ref[channel * RIM : (channel + 1) * RIM, :] = across_ref[
            channel, band_rows - RIM : band_rows, :
        ]


def warp_columns(pieces, shifts, width):
    _, _, band_rows, _ = pieces.shape
    rim = jax.ShapeDtypeStruct((4 * RIM, width), jnp.float32)
    return pl.pallas_call(
        across_kernel,
        out_shape=(jax.ShapeDtypeStruct((4, band_rows, width), jnp.float32), rim, rim),
        compiler_params=pltpu.CompilerParams(vmem_limit_bytes=VMEM_LIMIT),
    )(pieces, shifts)


def final_kernel(across_ref, low_ref, high_ref, shifts_ref, final_ref, extended):
    _, band_rows, width = across_ref.shape
    for channel in range(4):
        extended[channel, 16 : 16 + band_rows, :] = across_ref[channel]
        rim = slice(channel * RIM, (channel + 1) * RIM)
        extended[channel, 16 - RIM : 16, :] = low_ref[rim, :]
        extended[channel, 16 + band_rows : 16 + band_rows + RIM, :] = high_ref[rim, :]
    for lane in range(0, width, 128):
        lanes = slice(lane, lane + 128)
        shifts = jnp.broadcast_to(shifts_ref[:, lanes], (8, 128))
        factors = [weight_of(offset - shifts) for offset in range(-RIM, RIM + 1)]
        for channel in range(4):
            for row in range(0, band_rows, 8):
                result = jnp.zeros((8, 128), jnp.float32)
                for offset in range(-RIM, RIM + 1):
                    start = 16 + row + offset
                    result = result + factors[offset + RIM] * extended[
                        channel, start : start + 8, lanes
                    ]
                final_ref[channel, row : row + 8, lanes] = result


def warp_rows_of(across, low, high, shifts):
    _, band_rows, width = across.shape
    return pl.pallas_call(
        final_kernel,
        out_shape=jax.ShapeDtypeStruct(across.shape, jnp.float32),
        scratch_shapes=[pltpu.VMEM((4, band_rows + 32, width), jnp.float32)],
        compiler_params=pltpu.CompilerParams(vmem_limit_bytes=VMEM_LIMIT),
    )(across, low, high, shifts)


def neighbours(axis):
    count = lax.axis_size(axis)
    forward = [(i, i + 1) for i in range(count - 1)]
    return forward, [(target, source) for source, target in forward]


def per_device(volume, shear_rows, shear_cols, warp_cols, warp_rows):
    band_rows = volume.shape[2]
    columns = volume.shape[3]
    tiles = lax.axis_size("depth")
    width = columns // tiles
    forward, backward = neighbours("rows")
    up, down = pack_halo(volume, shear_rows)
    high = lax.ppermute(up, "rows", backward)
    low = lax.ppermute(down, "rows", forward)
    image = shear_slab(volume, shear_rows, shear_cols, low, high, tiles)
    pieces = lax.all_to_all(image, "depth", 0, 0, tiled=True)
    row_start = lax.axis_index("rows") * band_rows
    row_shifts = lax.dynamic_slice_in_dim(warp_cols, row_start, band_rows, 0)
    across, top, bottom = warp_columns(pieces, row_shifts[:, None], width)
    below = lax.ppermute(bottom, "rows", forward)
    above = lax.ppermute(top, "rows", backward)
    return warp_rows_of(across, below, above, warp_rows[None, :])


def solution(mesh):
    return jax.shard_map(
        per_device,
        mesh=mesh,
        in_specs=(P(None, "depth", "rows", None), P("depth"), P("depth"), P(), P("depth")),
        out_specs=P(None, "rows", "depth"),
        check_vma=False,
    )
```

time: 522 us -> 302 us (0.58); the launches traced: 516 us -> 306 us
  other arithmetic: 201 us -> 0 us
  Pallas kernels: 0 us -> 147 us
  loops' own time: 111 us -> 0 us
  local copies, waits for them, and re-layouts: 60.5 us -> 2.5 us
  starting transfers between devices: 19.6 us -> 27.2 us
    pallas_call x0 -> x4, Pallas kernels: none -> 147 us  [the longest x1 122 us: shear_slab(): pl.pallas_call(shear_kernel, out_shape=jax.ShapeDtypeStruct(image, jnp.bf...]
    another operation x1 -> x0, loops' own time: 111 us -> none  [per_device(): lax.fori_loop(0, slab_count, add_slice, jnp.zeros((4, band_rows, band_col...]
    add x34 -> x0, other arithmetic: 88.4 us -> none  [the longest x16 72.7 us: over_front(): return front_part + (1.0 - front_part[3:4]) * back_part]
    concatenate x17 -> x0, other arithmetic: 38.4 us -> none  [the longest x1 21.8 us: extended_2(): block = jnp.concatenate([low, block, high], axis=dim)]
    convert_element_type x22 -> x0, other arithmetic: 34.7 us -> none  [the longest x16 30.7 us: add_slice(): slice_now.astype(jnp.float32)]
    while x16 -> x0, other arithmetic: 26.3 us -> none
    dynamic_slice x32 -> x0, local copies, waits for them, and re-layouts: 18.9 us -> none  [the longest x16 9.52 us: add_slice(): shear_cols[index]]
    all_to_all x0 -> x1, waiting for transfers between devices: none -> 18 us  [per_device(): pieces = lax.all_to_all(image, 'depth', 0, 0, tiled=True)]
  transfers between devices with their start and end apart: 9 -> 5, of which waited for: 8 -> 5; matrix products, arithmetic and copies ran while one was open for 3% -> 0% of each run, Pallas kernels for 0% -> 0%
where the time goes in v1:
time: 302 us; the launch traced here: 306 us
  Pallas kernels  147 us (49%)
  waiting for transfers between devices  129 us (43%)
  starting transfers between devices  27.2 us (9%)
    pallas_call x1, Pallas kernels, shear_slab(): pl.pallas_call(shear_kernel, out_shape=jax.ShapeDtypeStruct(image, jnp.bf...  122 us
    ppermute x1, waiting for transfers between devices, per_device(): low = lax.ppermute(down, 'rows', forward)  101 us
    pallas_call x1, Pallas kernels, pack_halo(): pl.pallas_call(pack_kernel, out_shape=(packed, packed), grid_spec=pltpu.P...  18.6 us
    all_to_all x1, waiting for transfers between devices, per_device(): pieces = lax.all_to_all(image, 'depth', 0, 0, tiled=True)  18 us
    all_to_all x1, starting transfers between devices, per_device(): pieces = lax.all_to_all(image, 'depth', 0, 0, tiled=True)  15.5 us
  transfers between devices with their start and end apart: 5, of which 5 were waited for; matrix products, arithmetic and copies ran while one was open for 0% of the time, Pallas kernels for 0%

profile of v1, /device:TPU:24, one launch (start us, length us, event | category | flops | bytes accessed | tf_op | source)
XLA Modules:
  0.0 305.6 jit_solution(8270850381363486788)
XLA Ops:
  0.0 0.0 copy-start
  0.0 18.6 %shard_map.55 = (bf16[18,4,8,4096]{3,2,1,0:T(8,128)(2,1)}, bf16[18,4,8,4096]{3,2,1,0:T(8,128)(2,1)}) custom-call(s32[16]{0:T(128)} %shear_rows.3, bf16[4,16,32,4096]{3,2,1,0:T(8,128)(2,1)} %volume_ref.1, bf16[4,16,32,4096]{3,2,1,0:T(8,128)(2,1)} %volume_ref.1), custom_call_target="tpu_custom_call" | custom-call | tf_op jit(solution)/shard_map/pallas_call | solution.py:85
  18.6 3.5 %collective-permute-start = (bf16[18,4,8,4096]{3,2,1,0:T(8,128)(2,1)}, bf16[18,4,8,4096]{3,2,1,0:T(8,128)(2,1)}, u32[]{:S(2)}, u32[]{:S(2)}) collective-permute-start(bf16[18,4,8,4096]{3,2,1,0:T(8,128)(2,1)} %get-tuple-element.10), channel_id=1, source_target_pairs={{0,1},{1,2},{2,3},{3,4},{4,5},{5,6},{6,7},{7,8},{8,9},{9,10},{10,1... | collective-permute-start | bytes 14155784 | tf_op jit(solution)/shard_map/ppermute | solution.py:390
  22.1 2.4 collective-permute-start.1
  24.5 100.6 %collective-permute-done.low_ref = bf16[18,4,8,4096]{3,2,1,0:T(8,128)(2,1)} collective-permute-done((bf16[18,4,8,4096]{3,2,1,0:T(8,128)(2,1)}, bf16[18,4,8,4096]{3,2,1,0:T(8,128)(2,1)}, u32[]{:S(2)}, u32[]{:S(2)}) %collective-permute-start) | collective-permute-done | bytes 4718624 | tf_op jit(solution)/shard_map/ppermute | solution.py:390
  125.1 5.3 %collective-permute-done.1.high_ref = bf16[18,4,8,4096]{3,2,1,0:T(8,128)(2,1)} collective-permute-done((bf16[18,4,8,4096]{3,2,1,0:T(8,128)(2,1)}, bf16[18,4,8,4096]{3,2,1,0:T(8,128)(2,1)}, u32[]{:S(2)}, u32[]{:S(2)}) %collective-permute-start.1) | collective-permute-done | bytes 4718624 | tf_op jit(solution)/shard_map/ppermute | solution.py:389
  130.4 122.1 %shard_map.56 = bf16[8,4,32,640]{3,2,1,0:T(8,128)(2,1)} custom-call(s32[16]{0:T(128)} %shear_rows.3, s32[16]{0:T(128)} %shear_cols.1, bf16[4,16,32,4096]{3,2,1,0:T(8,128)(2,1)} %volume_ref.1, bf16[18,4,8,4096]{3,2,1,0:T(8,128)(2,1)} %collective-permute-done.low_ref, bf16[18,4,8,4096]{3,2,1,0:T(8,128)(2,1)} %collective-permute-done.1.high_ref), custom_call_target="tpu_custom_call" | custom-call | tf_op jit(solution)/shard_map/pallas_call | solution.py:272
  252.5 15.5 %all-to-all-start = ((bf16[8,4,32,640]{3,2,1,0:T(8,128)(2,1)}), bf16[8,4,32,640]{3,2,1,0:T(8,128)(2,1)S(1)}, u32[]{:S(2)}, u32[]{:S(2)}) async-start(bf16[8,4,32,640]{3,2,1,0:T(8,128)(2,1)} %shard_map.56), calls=%async_computation | async-start | bytes 2621440 | tf_op jit(solution)/shard_map/all_to_all | solution.py:392
  268.0 0.0 copy-done
  268.0 0.1 dynamic-slice_bitcast_fusion
  268.1 0.7 copy.6.shifts_ref
  268.8 18.0 %all-to-all-done.pieces_ref = bf16[8,4,32,640]{3,2,1,0:T(8,128)(2,1)S(1)} async-done(((bf16[8,4,32,640]{3,2,1,0:T(8,128)(2,1)}), bf16[8,4,32,640]{3,2,1,0:T(8,128)(2,1)S(1)}, u32[]{:S(2)}, u32[]{:S(2)}) %all-to-all-start) | async-done | bytes 1310752 | tf_op jit(solution)/shard_map/all_to_all | solution.py:392
  286.8 0.0 copy-start.1
  286.8 1.1 copy-done.1
  287.9 3.7 %shard_map.57 = (f32[4,32,512]{2,1,0:T(8,128)}, f32[36,512]{1,0:T(8,128)}, f32[36,512]{1,0:T(8,128)}) custom-call(bf16[8,4,32,640]{3,2,1,0:T(8,128)(2,1)} %copy-done.1, s32[32,1]{1,0:T(8,128)} %copy.6.shifts_ref), custom_call_target="tpu_custom_call" | custom-call | tf_op jit(solution)/shard_map/pallas_call | solution.py:337
  291.6 1.9 collective-permute-start.2
  293.5 3.9 %collective-permute-start.3 = (f32[36,512]{1,0:T(8,128)}, f32[36,512]{1,0:T(8,128)S(1)}, u32[]{:S(2)}, u32[]{:S(2)}) collective-permute-start(f32[36,512]{1,0:T(8,128)} %get-tuple-element.14), channel_id=1, source_target_pairs={{1,0},{2,1},{3,2},{4,3},{5,4},{6,5},{7,6},{8,7},{9,8},{10,9},{11,1... | collective-permute-start | bytes 221192 | tf_op jit(solution)/shard_map/ppermute | solution.py:397
  297.4 0.7 collective-permute-done.2.low_ref
  298.1 0.0 copy-start.2
  298.1 4.0 %collective-permute-done.3.high_ref = f32[36,512]{1,0:T(8,128)S(1)} collective-permute-done((f32[36,512]{1,0:T(8,128)}, f32[36,512]{1,0:T(8,128)S(1)}, u32[]{:S(2)}, u32[]{:S(2)}) %collective-permute-start.3) | collective-permute-done | bytes 73760 | tf_op jit(solution)/shard_map/ppermute | solution.py:397
  302.2 0.0 copy-start.3
  302.2 0.0 copy-done.2
  302.2 0.6 copy-done.3
  302.8 2.8 shard_map.58
Async XLA Ops:
  0.0 268.0 %copy-start = (s32[512]{0:T(512)S(1)}, s32[512]{0:T(512)}, u32[]{:S(2)}) copy-start(s32[512]{0:T(512)} %param.8) | copy-start | bytes 6148
  18.6 106.4 %collective-permute-start = (bf16[18,4,8,4096]{3,2,1,0:T(8,128)(2,1)}, bf16[18,4,8,4096]{3,2,1,0:T(8,128)(2,1)}, u32[]{:S(2)}, u32[]{:S(2)}) collective-permute-start(bf16[18,4,8,4096]{3,2,1,0:T(8,128)(2,1)} %get-tuple-element.10), channel_id=1, source_target_pairs={{0,1},{1,2},{2,3},{3,4},{4,5},{5,6},{6,7},{7,8},{8,9},{9,10},{10,1... | collective-permute-start | bytes 14155784 | tf_op jit(solution)/shard_map/ppermute | solution.py:390
  22.1 108.3 %collective-permute-start.1 = (bf16[18,4,8,4096]{3,2,1,0:T(8,128)(2,1)}, bf16[18,4,8,4096]{3,2,1,0:T(8,128)(2,1)}, u32[]{:S(2)}, u32[]{:S(2)}) collective-permute-start(bf16[18,4,8,4096]{3,2,1,0:T(8,128)(2,1)} %get-tuple-element.11), channel_id=1, source_target_pairs={{1,0},{2,1},{3,2},{4,3},{5,4},{6,5},{7,6},{8,7},{9,8},{10,9},{11,1... | collective-permute-start | bytes 14155784 | tf_op jit(solution)/shard_map/ppermute | solution.py:389
  252.5 34.3 %all-to-all-start = ((bf16[8,4,32,640]{3,2,1,0:T(8,128)(2,1)}), bf16[8,4,32,640]{3,2,1,0:T(8,128)(2,1)S(1)}, u32[]{:S(2)}, u32[]{:S(2)}) async-start(bf16[8,4,32,640]{3,2,1,0:T(8,128)(2,1)} %shard_map.56), calls=%async_computation | async-start | bytes 2621440 | tf_op jit(solution)/shard_map/all_to_all | solution.py:392
  286.8 1.1 copy-start.1
  291.6 6.5 %collective-permute-start.2 = (f32[36,512]{1,0:T(8,128)}, f32[36,512]{1,0:T(8,128)S(1)}, u32[]{:S(2)}, u32[]{:S(2)}) collective-permute-start(f32[36,512]{1,0:T(8,128)} %get-tuple-element.13), channel_id=1, source_target_pairs={{0,1},{1,2},{2,3},{3,4},{4,5},{5,6},{6,7},{7,8},{8,9},{9,10},{10,1... | collective-permute-start | bytes 221192 | tf_op jit(solution)/shard_map/ppermute | solution.py:396
  293.5 8.7 %collective-permute-start.3 = (f32[36,512]{1,0:T(8,128)}, f32[36,512]{1,0:T(8,128)S(1)}, u32[]{:S(2)}, u32[]{:S(2)}) collective-permute-start(f32[36,512]{1,0:T(8,128)} %get-tuple-element.14), channel_id=1, source_target_pairs={{1,0},{2,1},{3,2},{4,3},{5,4},{6,5},{7,6},{8,7},{9,8},{10,9},{11,1... | collective-permute-start | bytes 221192 | tf_op jit(solution)/shard_map/ppermute | solution.py:397
  298.1 4.0 %copy-start.2 = (f32[36,512]{1,0:T(8,128)}, f32[36,512]{1,0:T(8,128)S(1)}, u32[]{:S(2)}) copy-start(f32[36,512]{1,0:T(8,128)S(1)} %collective-permute-done.2.low_ref) | copy-start | bytes 221188
  302.2 0.6 copy-start.3

commit v2 on v1

--- a/solution.py
+++ b/solution.py
@@ -10,6 +10,10 @@
 SHIFT = 8
 RIM = SHIFT + 1
 BLOCK = 256
+GROUP = 16
+UNROLL = 1
+LEAST = 4
+STEP = 2
 EDGE = 128
 VMEM_LIMIT = 60 * 1024 * 1024
 
@@ -105,7 +109,7 @@
 
 def shear_kernel(
     shear_rows, shear_cols, volume_ref, low_ref, high_ref, image_ref,
-    inner, rim_low, rim_high, weights, filtered, total, used,
+    inner, rim, weights, filtered, total, used,
 ):
     index = pl.program_id(0)
     band_rows = volume_ref.shape[2]
@@ -119,9 +123,10 @@
     def _():
         used[0] = 0
         used[1] = 0
-        for part in (inner, rim_low, rim_high):
-            part[:, 0:EDGE] = jnp.zeros((part.shape[0], EDGE), jnp.bfloat16)
-            part[:, EDGE + columns :] = jnp.zeros((part.shape[0], EDGE), jnp.bfloat16)
+        for part in (inner, rim):
+            none = jnp.zeros((part.shape[1], EDGE), jnp.bfloat16)
+            part[0, :, 0:EDGE] = none
+            part[blocks, :, EDGE:] = none
 
         def clear(block, carry):
             start = pl.multiple_of(block * BLOCK, BLOCK)
@@ -151,96 +156,92 @@
         distance == 0, 0.125, jnp.where(distance == 1, 0.0625, 0.0)
     ).astype(jnp.bfloat16)
 
-    def premultiply(block, carry):
-        start = pl.multiple_of(block * BLOCK, BLOCK)
-        place = pl.multiple_of(start + EDGE, EDGE)
-        opacity = volume_ref[3, 0, :, pl.ds(start, BLOCK)].astype(jnp.float32)
-        for channel in range(4):
-            value = volume_ref[channel, 0, :, pl.ds(start, BLOCK)].astype(jnp.float32)
-            if channel < 3:
-                value = value * opacity
-            inner[pl.ds(channel * band_rows, band_rows), pl.ds(place, BLOCK)] = value.astype(
-                jnp.bfloat16
+    def premultiply(load, part, count):
+        def rows_at(block, lanes, start, size):
+            opacity = load(3, start, size)
+            for channel in range(4):
+                value = load(channel, start, size)
+                if channel < 3:
+                    value = value * opacity
+                part[block, channel * count : (channel + 1) * count, lanes] = value.astype(
+                    jnp.bfloat16
+                )
+
+        def body(block, carry):
+            start = pl.multiple_of(block * BLOCK - EDGE, EDGE)
+            rows_at(block, slice(0, BLOCK), start, BLOCK)
+            return carry
+
+        rows_at(0, slice(EDGE, BLOCK), 0, EDGE)
+        rows_at(blocks, slice(0, EDGE), columns - EDGE, EDGE)
+        lax.fori_loop(1, blocks, body, 0)
+
+    def filter_columns(part, count, row):
+        def body(step, carry):
+            first = step * GROUP
+            lhs0 = part[pl.ds(first, GROUP)].reshape(GROUP * 4 * count, BLOCK)
+            lhs1 = part[pl.ds(first + 1, GROUP)].reshape(GROUP * 4 * count, BLOCK)
+            rows = jnp.dot(
+                lhs0, weights[0:BLOCK, :], preferred_element_type=jnp.float32
+            ) + jnp.dot(lhs1, weights[BLOCK:, :], preferred_element_type=jnp.float32)
+            for block in range(GROUP):
+                for channel in range(4):
+                    top = (block * 4 + channel) * count
+                    for half in range(2):
+                        filtered[(first + block) * 2 + half, channel, pl.ds(row, count), :] = rows[
+                            top : top + count, half * 128 : half * 128 + 128
+                        ]
+            return carry
+
+        lax.fori_loop(0, blocks // GROUP, body, 0)
+
+    def rim_of(packed, group, row):
+        def load(channel, start, size):
+            return jnp.concatenate(
+                [
+                    packed[group + half, channel, :, pl.ds(start, size)].astype(jnp.float32)
+                    for half in range(2)
+                ],
+                0,
             )
+
+        premultiply(load, rim, 16)
+        filter_columns(rim, 16, row)
+
+    @pl.when(low_count > 0)
+    def _():
+        rim_of(low_ref, low_group, low_row)
+
+    @pl.when(high_count > 0)
+    def _():
+        rim_of(high_ref, high_group, high_row)
+
+    premultiply(
+        lambda channel, start, size: volume_ref[channel, 0, :, pl.ds(start, size)].astype(
+            jnp.float32
+        ),
+        inner,
+        band_rows,
+    )
+    filter_columns(inner, band_rows, 16)
+
+    def composite(tile, carry):
+        lanes = pl.ds(pl.multiple_of(tile * 128, 128), 128)
+
+        def sheared(channel):
+            first, middle, last = (
+                filtered[tile, channel, pl.ds(16 + row_shift + offset, band_rows), :]
+                for offset in (-1, 0, 1)
+            )
+            return first + last + (middle + middle)
+
+        passed = total[3, :, lanes]
+        for channel in range(3):
+            total[channel, :, lanes] = total[channel, :, lanes] + passed * sheared(channel)
+        total[3, :, lanes] = passed - passed * sheared(3)
         return carry
 
-    lax.fori_loop(0, blocks, premultiply, 0)
-
-    def premultiply_rim(packed, group, rim):
-        def body(block, carry):
-            start = pl.multiple_of(block * BLOCK, BLOCK)
-            place = pl.multiple_of(start + EDGE, EDGE)
-
-            def rows_of(channel):
-                return jnp.concatenate(
-                    [packed[group + half, channel, :, pl.ds(start, BLOCK)].astype(jnp.float32) for half in range(2)], 0
-                )
-
-            opacity = rows_of(3)
-            for channel in range(4):
-                value = rows_of(channel) * opacity if channel < 3 else opacity
-                rim[pl.ds(channel * 16, 16), pl.ds(place, BLOCK)] = value.astype(jnp.bfloat16)
-            return carry
-
-        lax.fori_loop(0, blocks, body, 0)
-
-    @pl.when(low_count > 0)
-    def _():
-        premultiply_rim(low_ref, low_group, rim_low)
-
-    @pl.when(high_count > 0)
-    def _():
-        premultiply_rim(high_ref, high_group, rim_high)
-
-    def filter_columns(part, start):
-        return jnp.dot(
-            part[:, pl.ds(start, 2 * BLOCK)], weights[...], preferred_element_type=jnp.float32
-        )
-
-    def composite(block, carry):
-        start = pl.multiple_of(block * BLOCK, BLOCK)
-
-        @pl.when(low_count > 0)
-        def _():
-            rows = filter_columns(rim_low, start)
-            for channel in range(4):
-                for tile in range(BLOCK // 128):
-                    filtered[tile, channel, pl.ds(low_row, 16), :] = rows[
-                        channel * 16 : channel * 16 + 16, tile * 128 : tile * 128 + 128
-                    ]
-
-        @pl.when(high_count > 0)
-        def _():
-            rows = filter_columns(rim_high, start)
-            for channel in range(4):
-                for tile in range(BLOCK // 128):
-                    filtered[tile, channel, pl.ds(high_row, 16), :] = rows[
-                        channel * 16 : channel * 16 + 16, tile * 128 : tile * 128 + 128
-                    ]
-
-        rows = filter_columns(inner, start)
-        for channel in range(4):
-            for tile in range(BLOCK // 128):
-                filtered[tile, channel, 16 : 16 + band_rows, :] = rows[
-                    channel * band_rows : (channel + 1) * band_rows, tile * 128 : tile * 128 + 128
-                ]
-        for tile in range(BLOCK // 128):
-            lanes = pl.ds(pl.multiple_of(start + tile * 128, 128), 128)
-
-            def sheared(channel):
-                first, middle, last = (
-                    filtered[tile, channel, pl.ds(16 + row_shift + offset, band_rows), :]
-                    for offset in (-1, 0, 1)
-                )
-                return first + last + (middle + middle)
-
-            passed = total[3, :, lanes]
-            for channel in range(3):
-                total[channel, :, lanes] = total[channel, :, lanes] + passed * sheared(channel)
-            total[3, :, lanes] = passed - passed * sheared(3)
-        return carry
-
-    lax.fori_loop(0, blocks, composite, 0)
+    lax.fori_loop(0, columns // 128, composite, 0, unroll=UNROLL)
 
     @pl.when(index == pl.num_programs(0) - 1)
     def _():
@@ -282,11 +283,10 @@
             ],
             out_specs=pl.BlockSpec(image, lambda i, a, b: (0, 0, 0, 0), pipeline_mode=pl.Buffered(1)),
             scratch_shapes=[
-                pltpu.VMEM((4 * band_rows, columns + 2 * EDGE), jnp.bfloat16),
-                pltpu.VMEM((64, columns + 2 * EDGE), jnp.bfloat16),
-                pltpu.VMEM((64, columns + 2 * EDGE), jnp.bfloat16),
+                pltpu.VMEM((columns // BLOCK + 1, 4 * band_rows, BLOCK), jnp.bfloat16),
+                pltpu.VMEM((columns // BLOCK + 1, 64, BLOCK), jnp.bfloat16),
                 pltpu.VMEM((2 * BLOCK, BLOCK), jnp.bfloat16),
-                pltpu.VMEM((BLOCK // 128, 4, band_rows + 32, 128), jnp.float32),
+                pltpu.VMEM((columns // 128, 4, band_rows + 32, 128), jnp.float32),
                 pltpu.VMEM((4, band_rows, columns), jnp.float32),
                 pltpu.SMEM((2,), jnp.int32),
             ],
@@ -386,9 +386,24 @@
     width = columns // tiles
     forward, backward = neighbours("rows")
     up, down = pack_halo(volume, shear_rows)
-    high = lax.ppermute(up, "rows", backward)
-    low = lax.ppermute(down, "rows", forward)
-    image = shear_slab(volume, shear_rows, shear_cols, low, high, tiles)
+    most = up.shape[0]
+    needed = jnp.maximum(
+        jnp.sum(rows_from_high(shear_rows)), jnp.sum(rows_from_low(shear_rows))
+    )
+    sizes = list(range(LEAST, most, STEP)) + [most]
+
+    def with_groups(groups):
+        def branch(up, down, volume, shear_rows, shear_cols):
+            high = lax.ppermute(up[:groups], "rows", backward)
+            low = lax.ppermute(down[most - groups :], "rows", forward)
+            return shear_slab(volume, shear_rows, shear_cols, low, high, tiles)
+
+        return branch
+
+    choice = jnp.clip((needed + (STEP * 8 - 1) - LEAST * 8) // (STEP * 8), 0, len(sizes) - 1)
+    image = lax.switch(
+        choice, [with_groups(groups) for groups in sizes], up, down, volume, shear_rows, shear_cols
+    )
     pieces = lax.all_to_all(image, "depth", 0, 0, tiled=True)
     row_start = lax.axis_index("rows") * band_rows
     row_shifts = lax.dynamic_slice_in_dim(warp_cols, row_start, band_rows, 0)

time: 302 us -> 166 us (0.55)
  Pallas kernels: 147 us -> 72.2 us
  waiting for transfers between devices: 129 us -> 65.1 us
  starting transfers between devices: 27.2 us -> 20.5 us
  local copies, waits for them, and re-layouts: 2.5 us -> 7.35 us
    pallas_call x1, Pallas kernels: 122 us -> 46.8 us  [shear_slab(): pl.pallas_call(shear_kernel, out_shape=jax.ShapeDtypeStruct(image, jnp.bf...]
    ppermute x2, waiting for transfers between devices: 106 us -> 42.4 us  [the longest x1 35.6 us: branch(): low = lax.ppermute(down[most - groups:], 'rows', forward)]
    all_to_all x1, starting transfers between devices: 15.5 us -> 8.81 us  [per_device(): pieces = lax.all_to_all(image, 'depth', 0, 0, tiled=True)]
    slice x0 -> x2, local copies, waits for them, and re-layouts: none -> 3.46 us  [the longest x1 1.73 us: branch(): low = lax.ppermute(down[most - groups:], 'rows', forward)]
  transfers between devices with their start and end apart: 5 -> 5, of which waited for: 5 -> 5; matrix products, arithmetic and copies ran while one was open for 0% -> 1% of each run, Pallas kernels for 0% -> 0%
where the time goes in v2:
time: 166 us; the launch traced here: 168 us
  Pallas kernels  72.2 us (43%)
  waiting for transfers between devices  65.1 us (39%)
  starting transfers between devices  20.5 us (12%)
  local copies, waits for them, and re-layouts  7.35 us (4%)
    pallas_call x1, Pallas kernels, shear_slab(): pl.pallas_call(shear_kernel, out_shape=jax.ShapeDtypeStruct(image, jnp.bf...  46.8 us
    ppermute x1, waiting for transfers between devices, branch(): low = lax.ppermute(down[most - groups:], 'rows', forward)  35.6 us
    pallas_call x1, Pallas kernels, pack_halo(): pl.pallas_call(pack_kernel, out_shape=(packed, packed), grid_spec=pltpu.P...  18.9 us
    all_to_all x1, waiting for transfers between devices, per_device(): pieces = lax.all_to_all(image, 'depth', 0, 0, tiled=True)  18 us
    all_to_all x1, starting transfers between devices, per_device(): pieces = lax.all_to_all(image, 'depth', 0, 0, tiled=True)  8.81 us
    ppermute x1, waiting for transfers between devices, branch(): high = lax.ppermute(up[:groups], 'rows', backward)  6.84 us
    ppermute x1, waiting for transfers between devices, per_device(): above = lax.ppermute(top, 'rows', backward)  4.03 us
    ppermute x1, starting transfers between devices, per_device(): above = lax.ppermute(top, 'rows', backward)  3.92 us
  transfers between devices with their start and end apart: 5, of which 5 were waited for; matrix products, arithmetic and copies ran while one was open for 1% of the time, Pallas kernels for 0%

profile of v2, /device:TPU:24, one launch (start us, length us, event | category | flops | bytes accessed | tf_op | source)
XLA Modules:
  0.0 168.0 jit_solution(4678241411065501776)
XLA Ops:
  0.0 1.4 maximum_reduce_fusion
  2.7 0.0 copy-start.17
  2.8 18.9 %shard_map.55 = (bf16[18,4,8,4096]{3,2,1,0:T(8,128)(2,1)}, bf16[18,4,8,4096]{3,2,1,0:T(8,128)(2,1)}) custom-call(s32[16]{0:T(128)} %shear_rows.1, bf16[4,16,32,4096]{3,2,1,0:T(8,128)(2,1)} %bottom_ref.1, bf16[4,16,32,4096]{3,2,1,0:T(8,128)(2,1)} %bottom_ref.1), custom_call_target="tpu_custom_call" | custom-call | tf_op jit(solution)/shard_map/pallas_call | solution.py:89
  21.6 99.9 %conditional.1 = (bf16[8,4,32,640]{3,2,1,0:T(8,128)(2,1)}) conditional(s32[]{:T(128)} %clamp.3, (bf16[18,4,8,4096]{3,2,1,0:T(8,128)(2,1)}, bf16[18,4,8,4096]{3,2,1,0:T(8,128)(2,1)}, s32[16]{0:T(128)S(1)}, s32[16]{0:T(128)S(1)}, bf16[4,16,32,4096]{3,2,1,0:T(8,128)(2,1)}) %tuple.47, ...), branch_computations={%region_2.3_spmd, %region_3.4_spmd, %region_4.5_spmd, %region_5.6_... | conditional | bytes 77594768 | solution.py:404
  21.7 1.7 %slice.32 = bf16[8,4,8,4096]{3,2,1,0:T(8,128)(2,1)S(1)} slice(bf16[18,4,8,4096]{3,2,1,0:T(8,128)(2,1)} %get-tuple-element.107), slice={[10:18], [0:4], [0:8], [0:4096]} | slice | bytes 4194304 | tf_op jit(solution)/shard_map/cond/branch_2_fun/slice | solution.py:398
  23.4 3.5 %collective-permute-start.4 = (bf16[8,4,8,4096]{3,2,1,0:T(8,128)(2,1)S(1)}, bf16[8,4,8,4096]{3,2,1,0:T(8,128)(2,1)S(1)}, u32[]{:S(2)}, u32[]{:S(2)}) collective-permute-start(bf16[8,4,8,4096]{3,2,1,0:T(8,128)(2,1)S(1)} %slice.32), channel_id=1, source_target_pairs={{0,1},{1,2},{2,3},{3,4},{4,5},{5,6},{6,7},{7,8},{8,9},{9,10},{10,1... | collective-permute-start | bytes 6291464 | tf_op jit(solution)/shard_map/cond/branch_2_fun/ppermute | solution.py:398
  26.9 1.7 %slice.33 = bf16[8,4,8,4096]{3,2,1,0:T(8,128)(2,1)S(1)} slice(bf16[18,4,8,4096]{3,2,1,0:T(8,128)(2,1)} %get-tuple-element.108), slice={[0:8], [0:4], [0:8], [0:4096]} | slice | bytes 4194304 | tf_op jit(solution)/shard_map/cond/branch_2_fun/slice | solution.py:397
  28.6 2.4 %collective-permute-start.5 = (bf16[8,4,8,4096]{3,2,1,0:T(8,128)(2,1)S(1)}, bf16[8,4,8,4096]{3,2,1,0:T(8,128)(2,1)S(1)}, u32[]{:S(2)}, u32[]{:S(2)}) collective-permute-start(bf16[8,4,8,4096]{3,2,1,0:T(8,128)(2,1)S(1)} %slice.33), channel_id=1, source_target_pairs={{1,0},{2,1},{3,2},{4,3},{5,4},{6,5},{7,6},{8,7},{9,8},{10,9},{11,1... | collective-permute-start | bytes 6291464 | tf_op jit(solution)/shard_map/cond/branch_2_fun/ppermute | solution.py:397
  31.0 35.6 %collective-permute-done.4.low_ref = bf16[8,4,8,4096]{3,2,1,0:T(8,128)(2,1)S(1)} collective-permute-done((bf16[8,4,8,4096]{3,2,1,0:T(8,128)(2,1)S(1)}, bf16[8,4,8,4096]{3,2,1,0:T(8,128)(2,1)S(1)}, u32[]{:S(2)}, u32[]{:S(2)}) %collective-permute-start.4) | collective-permute-done | bytes 2097184 | tf_op jit(solution)/shard_map/cond/branch_2_fun/ppermute | solution.py:398
  66.6 6.8 %collective-permute-done.5.high_ref = bf16[8,4,8,4096]{3,2,1,0:T(8,128)(2,1)S(1)} collective-permute-done((bf16[8,4,8,4096]{3,2,1,0:T(8,128)(2,1)S(1)}, bf16[8,4,8,4096]{3,2,1,0:T(8,128)(2,1)S(1)}, u32[]{:S(2)}, u32[]{:S(2)}) %collective-permute-start.5) | collective-permute-done | bytes 2097184 | tf_op jit(solution)/shard_map/cond/branch_2_fun/ppermute | solution.py:397
  73.4 1.4 copy-done.10
  74.8 46.8 %branch_2_fun.1 = bf16[8,4,32,640]{3,2,1,0:T(8,128)(2,1)} custom-call(s32[16]{0:T(128)S(1)} %get-tuple-element.104.shear_rows, s32[16]{0:T(128)S(1)} %get-tuple-element.105.shear_cols, bf16[4,16,32,4096]{3,2,1,0:T(8,128)(2,1)} %get-tuple-element.106.volume_ref, bf16[8,4,8,4096]{3,2,1,0:T(8,128)(2,1)} %copy-done.9, bf16[8,4,8,4096]{3,2,1,0:T(8,128)(2,1)} %copy-done.10), custom_call_target="tpu_custom_call" | custom-call | tf_op jit(solution)/shard_map/cond/branch_2_fun/pallas_call | solution.py:273
  121.5 8.8 %all-to-all-start = ((bf16[8,4,32,640]{3,2,1,0:T(8,128)(2,1)}), bf16[8,4,32,640]{3,2,1,0:T(8,128)(2,1)S(1)}, u32[]{:S(2)}, u32[]{:S(2)}) async-start(bf16[8,4,32,640]{3,2,1,0:T(8,128)(2,1)} %get-tuple-element.146), calls=%async_computation | async-start | bytes 2621440 | tf_op jit(solution)/shard_map/all_to_all | solution.py:407
  130.4 0.1 dynamic-slice_bitcast_fusion
  130.4 0.7 copy.6.shifts_ref
  131.1 18.0 %all-to-all-done.pieces_ref = bf16[8,4,32,640]{3,2,1,0:T(8,128)(2,1)S(1)} async-done(((bf16[8,4,32,640]{3,2,1,0:T(8,128)(2,1)}), bf16[8,4,32,640]{3,2,1,0:T(8,128)(2,1)S(1)}, u32[]{:S(2)}, u32[]{:S(2)}) %all-to-all-start) | async-done | bytes 1310752 | tf_op jit(solution)/shard_map/all_to_all | solution.py:407
  149.1 1.1 copy-done.5
  150.2 3.8 %shard_map.56 = (f32[4,32,512]{2,1,0:T(8,128)}, f32[36,512]{1,0:T(8,128)}, f32[36,512]{1,0:T(8,128)}) custom-call(bf16[8,4,32,640]{3,2,1,0:T(8,128)(2,1)} %copy-done.5, s32[32,1]{1,0:T(8,128)} %copy.6.shifts_ref), custom_call_target="tpu_custom_call" | custom-call | tf_op jit(solution)/shard_map/pallas_call | solution.py:337
  154.0 1.9 %collective-permute-start.16 = (f32[36,512]{1,0:T(8,128)}, f32[36,512]{1,0:T(8,128)S(1)}, u32[]{:S(2)}, u32[]{:S(2)}) collective-permute-start(f32[36,512]{1,0:T(8,128)} %get-tuple-element.142), channel_id=1, source_target_pairs={{0,1},{1,2},{2,3},{3,4},{4,5},{5,6},{6,7},{7,8},{8,9},{9,10},{10,1... | collective-permute-start | bytes 221192 | tf_op jit(solution)/shard_map/ppermute | solution.py:411
  155.9 3.9 %collective-permute-start.17 = (f32[36,512]{1,0:T(8,128)}, f32[36,512]{1,0:T(8,128)S(1)}, u32[]{:S(2)}, u32[]{:S(2)}) collective-permute-start(f32[36,512]{1,0:T(8,128)} %get-tuple-element.143), channel_id=1, source_target_pairs={{1,0},{2,1},{3,2},{4,3},{5,4},{6,5},{7,6},{8,7},{9,8},{10,9},{11,1... | collective-permute-start | bytes 221192 | tf_op jit(solution)/shard_map/ppermute | solution.py:412
  159.9 0.7 collective-permute-done.16.low_ref
  160.5 4.0 %collective-permute-done.17.high_ref = f32[36,512]{1,0:T(8,128)S(1)} collective-permute-done((f32[36,512]{1,0:T(8,128)}, f32[36,512]{1,0:T(8,128)S(1)}, u32[]{:S(2)}, u32[]{:S(2)}) %collective-permute-start.17) | collective-permute-done | bytes 73760 | tf_op jit(solution)/shard_map/ppermute | solution.py:412
  164.6 0.6 copy-done.16
  165.2 2.8 %shard_map.57 = f32[4,32,512]{2,1,0:T(8,128)} custom-call(f32[4,32,512]{2,1,0:T(8,128)} %get-tuple-element.141.across_ref, f32[36,512]{1,0:T(8,128)} %copy-done.15, f32[36,512]{1,0:T(8,128)} %copy-done.16, s32[1,512]{1,0:T(1,128)} %bitcast.3), custom_call_target="tpu_custom_call" | custom-call | tf_op jit(solution)/shard_map/pallas_call | solution.py:368
  (12 shorter events, 0.0 us)
Async XLA Ops:
  0.0 130.4 %copy-start = (s32[512]{0:T(512)S(1)}, s32[512]{0:T(512)}, u32[]{:S(2)}) copy-start(s32[512]{0:T(512)} %param.16) | copy-start | bytes 6148
  2.7 18.9 %copy-start.17 = (s32[16]{0:T(128)S(1)}, s32[16]{0:T(128)}, u32[]{:S(2)}) copy-start(s32[16]{0:T(128)} %shear_rows.1) | copy-start | bytes 196
  2.7 18.9 %copy-start.18 = (s32[16]{0:T(128)S(1)}, s32[16]{0:T(128)}, u32[]{:S(2)}) copy-start(s32[16]{0:T(128)} %param.15) | copy-start | bytes 196
  23.4 43.2 %collective-permute-start.4 = (bf16[8,4,8,4096]{3,2,1,0:T(8,128)(2,1)S(1)}, bf16[8,4,8,4096]{3,2,1,0:T(8,128)(2,1)S(1)}, u32[]{:S(2)}, u32[]{:S(2)}) collective-permute-start(bf16[8,4,8,4096]{3,2,1,0:T(8,128)(2,1)S(1)} %slice.32), channel_id=1, source_target_pairs={{0,1},{1,2},{2,3},{3,4},{4,5},{5,6},{6,7},{7,8},{8,9},{9,10},{10,1... | collective-permute-start | bytes 6291464 | tf_op jit(solution)/shard_map/cond/branch_2_fun/ppermute | solution.py:398
  28.6 44.8 %collective-permute-start.5 = (bf16[8,4,8,4096]{3,2,1,0:T(8,128)(2,1)S(1)}, bf16[8,4,8,4096]{3,2,1,0:T(8,128)(2,1)S(1)}, u32[]{:S(2)}, u32[]{:S(2)}) collective-permute-start(bf16[8,4,8,4096]{3,2,1,0:T(8,128)(2,1)S(1)} %slice.33), channel_id=1, source_target_pairs={{1,0},{2,1},{3,2},{4,3},{5,4},{6,5},{7,6},{8,7},{9,8},{10,9},{11,1... | collective-permute-start | bytes 6291464 | tf_op jit(solution)/shard_map/cond/branch_2_fun/ppermute | solution.py:397
  66.6 8.2 %copy-start.9 = (bf16[8,4,8,4096]{3,2,1,0:T(8,128)(2,1)}, bf16[8,4,8,4096]{3,2,1,0:T(8,128)(2,1)S(1)}, u32[]{:S(2)}) copy-start(bf16[8,4,8,4096]{3,2,1,0:T(8,128)(2,1)S(1)} %collective-permute-done.4.low_ref) | copy-start | bytes 6291460 | tf_op jit(solution)/shard_map/cond
  73.4 1.4 copy-start.10
  121.5 27.6 %all-to-all-start = ((bf16[8,4,32,640]{3,2,1,0:T(8,128)(2,1)}), bf16[8,4,32,640]{3,2,1,0:T(8,128)(2,1)S(1)}, u32[]{:S(2)}, u32[]{:S(2)}) async-start(bf16[8,4,32,640]{3,2,1,0:T(8,128)(2,1)} %get-tuple-element.146), calls=%async_computation | async-start | bytes 2621440 | tf_op jit(solution)/shard_map/all_to_all | solution.py:407
  149.1 1.1 copy-start.5
  154.0 6.5 %collective-permute-start.16 = (f32[36,512]{1,0:T(8,128)}, f32[36,512]{1,0:T(8,128)S(1)}, u32[]{:S(2)}, u32[]{:S(2)}) collective-permute-start(f32[36,512]{1,0:T(8,128)} %get-tuple-element.142), channel_id=1, source_target_pairs={{0,1},{1,2},{2,3},{3,4},{4,5},{5,6},{6,7},{7,8},{8,9},{9,10},{10,1... | collective-permute-start | bytes 221192 | tf_op jit(solution)/shard_map/ppermute | solution.py:411
  155.9 8.7 %collective-permute-start.17 = (f32[36,512]{1,0:T(8,128)}, f32[36,512]{1,0:T(8,128)S(1)}, u32[]{:S(2)}, u32[]{:S(2)}) collective-permute-start(f32[36,512]{1,0:T(8,128)} %get-tuple-element.143), channel_id=1, source_target_pairs={{1,0},{2,1},{3,2},{4,3},{5,4},{6,5},{7,6},{8,7},{9,8},{10,9},{11,1... | collective-permute-start | bytes 221192 | tf_op jit(solution)/shard_map/ppermute | solution.py:412
  160.5 4.0 %copy-start.15 = (f32[36,512]{1,0:T(8,128)}, f32[36,512]{1,0:T(8,128)S(1)}, u32[]{:S(2)}) copy-start(f32[36,512]{1,0:T(8,128)S(1)} %collective-permute-done.16.low_ref) | copy-start | bytes 221188
  164.6 0.6 copy-start.16

commit v3 on v1

v3 whole, which is shorter than its diff:
```python
import functools

import jax
import jax.numpy as jnp
from jax import lax
from jax.experimental import pallas as pl
from jax.experimental.pallas import tpu as pltpu
from jax.sharding import PartitionSpec as P

SHIFT = 8
RIM = SHIFT + 1
BLOCK = 256
GROUP = 16
UNROLL = 2
PACK_UNROLL = 8
SIZES = (6, 7, 8, 9, 11)
ORDERED = False
EDGE = 128
VMEM_LIMIT = 60 * 1024 * 1024


def rows_from_high(shift):
    return jnp.maximum(shift + 1, 0)


def rows_from_low(shift):
    return jnp.maximum(1 - shift, 0)


def pack_kernel(
    shear_rows, volume_ref, up_first, up_second, down_first, down_second,
    up_tiles, down_tiles, up_rows, down_rows, up_out, down_out, in_sems, out_sems,
):
    early = up_first.shape[0]
    late = up_second.shape[0]
    groups = early + late
    slices = volume_ref.shape[1]
    band_rows = volume_ref.shape[2]
    tiles = up_first.shape[3] // 128

    def fetch(index, side, count, act):
        buffer = (up_tiles, down_tiles)[side]
        first = 0 if side == 0 else band_rows - count
        place = 0 if side == 0 else 16 - count
        copy = pltpu.make_async_copy(
            volume_ref.at[:, index, pl.ds(first, count), :],
            buffer.at[index, :, pl.ds(place, count), :],
            in_sems.at[side, index],
        )
        act(copy)

    def each_size(needed, act):
        @pl.when((needed > 0) & (needed <= 8))
        def _():
            act(8)

        @pl.when(needed > 8)
        def _():
            act(16)

    def start_slice(index, carry):
        shift = shear_rows[index]
        each_size(rows_from_high(shift), lambda n: fetch(index, 0, n, lambda c: c.start()))
        each_size(rows_from_low(shift), lambda n: fetch(index, 1, n, lambda c: c.start()))
        return carry

    lax.fori_loop(0, slices, start_slice, 0)

    def scatter(index, side, count, row):
        fetch(index, side, count, lambda c: c.wait())
        source = (up_tiles, down_tiles)[side]
        target = (up_rows, down_rows)[side]
        first = 0 if side == 0 else 16 - count

        def body(tile, carry):
            lane = pl.multiple_of(tile * 128, 128)
            for channel in range(4):
                target[tile, channel, pl.ds(row, count), :] = source[
                    index, channel, first : first + count, pl.ds(lane, 128)
                ].astype(jnp.float32)
            return carry

        lax.fori_loop(0, tiles, body, 0, unroll=PACK_UNROLL)

    def pack_slice(index, used):
        up_used, down_used = used
        shift = shear_rows[index]
        up_count = rows_from_high(shift)
        down_count = rows_from_low(shift)
        down_stop = groups * 8 + 16 - down_used
        each_size(up_count, lambda n: scatter(index, 0, n, up_used))
        each_size(down_count, lambda n: scatter(index, 1, n, down_stop - n))
        return up_used + up_count, down_used + down_count

    lax.fori_loop(0, slices, pack_slice, (0, 0))

    def flush(group, side):
        source = (up_rows, down_rows)[side]
        target = (up_out, down_out)[side]

        def body(tile, carry):
            lanes = pl.ds(pl.multiple_of(tile * 128, 128), 128)
            row = pl.multiple_of(group * 8 + 16 * side, 8)
            for channel in range(4):
                target[group, channel, :, lanes] = source[tile, channel, pl.ds(row, 8), :].astype(
                    jnp.bfloat16
                )
            return carry

        lax.fori_loop(0, tiles, body, 0, unroll=PACK_UNROLL)

    chunks = (
        (up_first, 0, 0, early),
        (down_first, 1, late, early),
        (up_second, 0, early, late),
        (down_second, 1, 0, late),
    )

    def send(target, side, group, first):
        source = (up_out, down_out)[side]
        return pltpu.make_async_copy(
            source.at[group], target.at[group - first], out_sems.at[side, group]
        )

    for target, side, first, count in chunks:

        def start(group, carry):
            flush(group, side)
            send(target, side, group, first).start()
            return carry

        lax.fori_loop(first, first + count, start, 0)
    for target, side, first, count in chunks:

        def finish(group, carry):
            send(target, side, group, first).wait()
            return carry

        lax.fori_loop(first, first + count, finish, 0)


def pack_halo(volume, shear_rows, early, late):
    _, slices, _, columns = volume.shape
    groups = early + late

    def packed(count):
        return jax.ShapeDtypeStruct((count, 4, 8, columns), jnp.bfloat16)

    tiles = pltpu.VMEM((slices, 4, 16, columns), jnp.bfloat16)
    rows = pltpu.VMEM((columns // 128, 4, groups * 8 + 16, 128), jnp.float32)
    out = pltpu.VMEM((groups, 4, 8, columns), jnp.bfloat16)
    return pl.pallas_call(
        pack_kernel,
        out_shape=(packed(early), packed(late), packed(early), packed(late)),
        grid_spec=pltpu.PrefetchScalarGridSpec(
            num_scalar_prefetch=1,
            grid=(1,),
            in_specs=[pl.BlockSpec(memory_space=pl.ANY)],
            out_specs=[pl.BlockSpec(memory_space=pl.ANY)] * 4,
            scratch_shapes=[
                tiles, tiles, rows, rows, out, out,
                pltpu.SemaphoreType.DMA((2, slices)),
                pltpu.SemaphoreType.DMA((2, groups)),
            ],
        ),
        compiler_params=pltpu.CompilerParams(vmem_limit_bytes=VMEM_LIMIT),
    )(shear_rows, volume)


def shear_kernel(part, *refs):
    shear_rows, shear_cols, bounds, volume_ref = refs[:4]
    if part == "front":
        low_refs, high_refs = [refs[4]], [refs[5]]
        before_ref, total, inner, rim, weights, filtered, halo, slabs, sems, slab_sems = None, *refs[6:]
    else:
        low_refs, high_refs = [refs[5], refs[4]], [refs[6], refs[7]]
        before_ref, image_ref, inner, rim, weights, filtered, halo, slabs, sems, slab_sems, total = refs[8:]
    begin = bounds[0]
    end = bounds[1]
    band_rows = volume_ref.shape[2]
    columns = volume_ref.shape[3]
    blocks = columns // BLOCK
    groups = halo.shape[1]
    stacked = min(GROUP, blocks)

    def fetch(index):
        slot = lax.rem(index - begin, 2)
        return pltpu.make_async_copy(volume_ref.at[:, index], slabs.at[slot], slab_sems.at[slot])

    copies = []
    for side, packed in enumerate((low_refs, high_refs)):
        first = 0
        for ref in packed:
            count = ref.shape[0]
            copies.append((ref, halo.at[side, pl.ds(first, count)]))
            first += count
    if before_ref is not None:
        copies.append((before_ref, total))
    copies = [
        pltpu.make_async_copy(source, target, sems.at[place])
        for place, (source, target) in enumerate(copies)
    ]

    fetch(begin).start()
    for copy in copies:
        copy.start()
    for edge in (inner, rim):
        none = jnp.zeros((edge.shape[1], EDGE), jnp.bfloat16)
        edge[0, :, 0:EDGE] = none
        edge[blocks, :, EDGE:] = none
    if before_ref is None:

        def clear(block, carry):
            start = pl.multiple_of(block * BLOCK, BLOCK)
            for channel in range(4):
                total[channel, :, pl.ds(start, BLOCK)] = jnp.full(
                    (band_rows, BLOCK), 0.0 if channel < 3 else 1.0, jnp.float32
                )
            return carry

        lax.fori_loop(0, blocks, clear, 0)

    def add(earlier, carry):
        shift = shear_rows[earlier]
        return carry[0] + rows_from_low(shift), carry[1] + rows_from_high(shift)

    def shear_slice(index, slot, used):
        row_shift = shear_rows[index]
        col_shift = shear_cols[index]
        low_count = rows_from_low(row_shift)
        high_count = rows_from_high(row_shift)
        low_start = groups * 8 - used[0] - low_count
        high_start = used[1]
        source = lax.broadcasted_iota(jnp.int32, (2 * BLOCK, BLOCK), 0)
        target = lax.broadcasted_iota(jnp.int32, (2 * BLOCK, BLOCK), 1)
        distance = jnp.abs(source - target - EDGE - col_shift)
        weights[...] = jnp.where(
            distance == 0, 0.125, jnp.where(distance == 1, 0.0625, 0.0)
        ).astype(jnp.bfloat16)

        def premultiply(load, part, count):
            def rows_at(block, lanes, start, size):
                opacity = load(3, start, size)
                for channel in range(4):
                    value = load(channel, start, size)
                    if channel < 3:
                        value = value * opacity
                    part[block, channel * count : (channel + 1) * count, lanes] = value.astype(
                        jnp.bfloat16
                    )

            def body(block, carry):
                start = pl.multiple_of(block * BLOCK - EDGE, EDGE)
                rows_at(block, slice(0, BLOCK), start, BLOCK)
                return carry

            rows_at(0, slice(EDGE, BLOCK), 0, EDGE)
            rows_at(blocks, slice(0, EDGE), columns - EDGE, EDGE)
            lax.fori_loop(1, blocks, body, 0, unroll=3)

        def filter_columns(part, count, row):
            def body(step, carry):
                first = step * stacked
                lhs0 = part[pl.ds(first, stacked)].reshape(stacked * 4 * count, BLOCK)
                lhs1 = part[pl.ds(first + 1, stacked)].reshape(stacked * 4 * count, BLOCK)
                rows = jnp.dot(
                    lhs0, weights[0:BLOCK, :], preferred_element_type=jnp.float32
                ) + jnp.dot(lhs1, weights[BLOCK:, :], preferred_element_type=jnp.float32)
                for block in range(stacked):
                    for channel in range(4):
                        top = (block * 4 + channel) * count
                        for half in range(2):
                            filtered[(first + block) * 2 + half, channel, pl.ds(row, count), :] = rows[
                                top : top + count, half * 128 : half * 128 + 128
                            ]
                return carry

            lax.fori_loop(0, blocks // stacked, body, 0)

        premultiply(
            lambda channel, start, size: slabs[slot, channel, :, pl.ds(start, size)].astype(
                jnp.float32
            ),
            inner,
            band_rows,
        )

        @pl.when(index == begin)
        def _():
            for copy in copies:
                copy.wait()

        def rim_of(side, carry):
            packed_row = jnp.where(side == 0, low_start, high_start)
            group = jnp.minimum(packed_row // 8, groups - 2)
            place = jnp.where(side == 0, 16 - low_count, 16 + band_rows)

            def load(channel, start, size):
                return jnp.concatenate(
                    [
                        halo[side, group + half, channel, :, pl.ds(start, size)].astype(jnp.float32)
                        for half in range(2)
                    ],
                    0,
                )

            premultiply(load, rim, 16)
            filter_columns(rim, 16, place - (packed_row - group * 8))
            return carry

        lax.fori_loop(
            jnp.where(low_count > 0, 0, 1), jnp.where(high_count > 0, 2, 1), rim_of, 0
        )
        filter_columns(inner, band_rows, 16)

        def composite(tile, carry):
            lanes = pl.ds(pl.multiple_of(tile * 128, 128), 128)

            def sheared(channel):
                first, middle, last = (
                    filtered[tile, channel, pl.ds(16 + row_shift + offset, band_rows), :]
                    for offset in (-1, 0, 1)
                )
                return first + last + (middle + middle)

            passed = total[3, :, lanes]
            for channel in range(3):
                total[channel, :, lanes] = total[channel, :, lanes] + passed * sheared(channel)
            total[3, :, lanes] = passed - passed * sheared(3)
            return carry

        lax.fori_loop(0, columns // 128, composite, 0, unroll=UNROLL)

    def one_slice(index, used):
        fetch(index).wait()

        @pl.when(index + 1 < end)
        def _():
            fetch(index + 1).start()

        shear_slice(index, lax.rem(index - begin, 2), used)
        return add(index, used)

    lax.fori_loop(begin, end, one_slice, lax.fori_loop(0, begin, add, (0, 0)))
    if part == "back":
        emit_tiles(total, image_ref)


def emit_tiles(total, image_ref):
    _, band_rows, columns = total.shape
    tiles = image_ref.shape[0]
    width = columns // tiles
    lane = lax.broadcasted_iota(jnp.int32, (band_rows, EDGE), 1)

    def value(channel, start, size):
        part = total[channel, :, pl.ds(pl.multiple_of(start, EDGE), size)]
        return part if channel < 3 else 1.0 - part

    def body(tile, carry):
        first = tile * width
        for channel in range(4):
            image_ref[tile, channel, :, 0:width] = value(channel, first, width).astype(
                jnp.bfloat16
            )
            before = value(channel, jnp.maximum(first - EDGE, 0), EDGE)
            after = value(channel, jnp.minimum(first + width, columns - EDGE), EDGE)
            before = jnp.where(tile > 0, before, 0.0)
            after = jnp.where(tile < tiles - 1, after, 0.0)
            image_ref[tile, channel, :, width:] = jnp.where(
                lane < EDGE // 2, after, before
            ).astype(jnp.bfloat16)
        return carry

    lax.fori_loop(0, tiles, body, 0)


def shear_part(part, bounds, volume, shear_rows, shear_cols, packed, before, tiles):
    _, _, band_rows, columns = volume.shape
    groups = sum(chunk.shape[0] for chunk in packed) // 2

    outside = list(packed) + ([] if before is None else [before])
    total_shape = (4, band_rows, columns)
    scratch = [
        pltpu.VMEM((columns // BLOCK + 1, 4 * band_rows, BLOCK), jnp.bfloat16),
        pltpu.VMEM((columns // BLOCK + 1, 64, BLOCK), jnp.bfloat16),
        pltpu.VMEM((2 * BLOCK, BLOCK), jnp.bfloat16),
        pltpu.VMEM((columns // 128, 4, band_rows + 32, 128), jnp.float32),
        pltpu.VMEM((2, groups, 4, 8, columns), jnp.bfloat16),
        pltpu.VMEM((2, 4, band_rows, columns), jnp.bfloat16),
        pltpu.SemaphoreType.DMA((len(outside),)),
        pltpu.SemaphoreType.DMA((2,)),
    ]
    if part == "front":
        out = jax.ShapeDtypeStruct(total_shape, jnp.float32)
    else:
        image = (tiles, 4, band_rows, columns // tiles + EDGE)
        out = jax.ShapeDtypeStruct(image, jnp.bfloat16)
        scratch.append(pltpu.VMEM(total_shape, jnp.float32))
    whole = len(out.shape)
    return pl.pallas_call(
        functools.partial(shear_kernel, part),
        out_shape=out,
        grid_spec=pltpu.PrefetchScalarGridSpec(
            num_scalar_prefetch=3,
            grid=(1,),
            in_specs=[pl.BlockSpec(memory_space=pl.ANY)] * (1 + len(outside)),
            out_specs=pl.BlockSpec(
                out.shape, lambda i, a, b, c: (0,) * whole, pipeline_mode=pl.Buffered(1)
            ),
            scratch_shapes=scratch,
        ),
        compiler_params=pltpu.CompilerParams(vmem_limit_bytes=VMEM_LIMIT),
        cost_estimate=pl.CostEstimate(
            flops=2 * 512 * volume.size, transcendentals=0, bytes_accessed=volume.size
        ),
    )(shear_rows, shear_cols, bounds, volume, *outside)


def weight_of(offset):
    return jnp.where(offset == 0, 0.5, jnp.where(jnp.abs(offset) == 1, 0.25, 0.0))


def across_kernel(pieces_ref, shifts_ref, across_ref, top_ref, bottom_ref):
    tiles, _, band_rows, padded = pieces_ref.shape
    width = across_ref.shape[2]
    for row in range(0, band_rows, 8):
        rows = slice(row, row + 8)
        totals = [None] * 4
        passed = None
        for tile in range(tiles):
            parts = [pieces_ref[tile, channel, rows, :].astype(jnp.float32) for channel in range(4)]
            if tile == 0:
                totals = parts[:3]
                passed = 1.0 - parts[3]
            else:
                totals = [total + passed * part for total, part in zip(totals, parts[:3])]
                passed = passed - passed * parts[3]
        totals = totals[:3] + [1.0 - passed]
        shifts = jnp.broadcast_to(shifts_ref[rows, :], (8, width))
        results = [jnp.zeros((8, width), jnp.float32)] * 4
        for offset in range(-RIM, RIM + 1):
            factor = weight_of(offset - shifts)
            for channel in range(4):
                moved = pltpu.roll(totals[channel], (-offset) % padded, 1)[:, :width]
                results[channel] = results[channel] + factor * moved
        for channel in range(4):
            across_ref[channel, rows, :] = results[channel]
    for channel in range(4):
        top_ref[channel * RIM : (channel + 1) * RIM, :] = across_ref[channel, 0:RIM, :]
        bottom_ref[channel * RIM : (channel + 1) * RIM, :] = across_ref[
            channel, band_rows - RIM : band_rows, :
        ]


def warp_columns(pieces, shifts, width):
    _, _, band_rows, _ = pieces.shape
    rim = jax.ShapeDtypeStruct((4 * RIM, width), jnp.float32)
    return pl.pallas_call(
        across_kernel,
        out_shape=(jax.ShapeDtypeStruct((4, band_rows, width), jnp.float32), rim, rim),
        compiler_params=pltpu.CompilerParams(vmem_limit_bytes=VMEM_LIMIT),
    )(pieces, shifts)


def final_kernel(across_ref, low_ref, high_ref, shifts_ref, final_ref, extended):
    _, band_rows, width = across_ref.shape
    for channel in range(4):
        extended[channel, 16 : 16 + band_rows, :] = across_ref[channel]
        rim = slice(channel * RIM, (channel + 1) * RIM)
        extended[channel, 16 - RIM : 16, :] = low_ref[rim, :]
        extended[channel, 16 + band_rows : 16 + band_rows + RIM, :] = high_ref[rim, :]
    for lane in range(0, width, 128):
        lanes = slice(lane, lane + 128)
        shifts = jnp.broadcast_to(shifts_ref[:, lanes], (8, 128))
        factors = [weight_of(offset - shifts) for offset in range(-RIM, RIM + 1)]
        for channel in range(4):
            for row in range(0, band_rows, 8):
                result = jnp.zeros((8, 128), jnp.float32)
                for offset in range(-RIM, RIM + 1):
                    start = 16 + row + offset
                    result = result + factors[offset + RIM] * extended[
                        channel, start : start + 8, lanes
                    ]
                final_ref[channel, row : row + 8, lanes] = result


def warp_rows_of(across, low, high, shifts):
    _, band_rows, width = across.shape
    return pl.pallas_call(
        final_kernel,
        out_shape=jax.ShapeDtypeStruct(across.shape, jnp.float32),
        scratch_shapes=[pltpu.VMEM((4, band_rows + 32, width), jnp.float32)],
        compiler_params=pltpu.CompilerParams(vmem_limit_bytes=VMEM_LIMIT),
    )(across, low, high, shifts)


def neighbours(axis):
    count = lax.axis_size(axis)
    forward = [(i, i + 1) for i in range(count - 1)]
    return forward, [(target, source) for source, target in forward]


def per_device(volume, shear_rows, shear_cols, warp_cols, warp_rows):
    band_rows = volume.shape[2]
    columns = volume.shape[3]
    tiles = lax.axis_size("depth")
    width = columns // tiles
    forward, backward = neighbours("rows")
    slices = volume.shape[1]
    most = -(-RIM * slices // 8)
    sizes = [size for size in SIZES if size < most] + [most]
    earlier = jnp.arange(slices)[None, :] <= jnp.arange(slices)[:, None]
    reach = jnp.maximum(
        jnp.sum(jnp.where(earlier, rows_from_high(shear_rows)[None, :], 0), 1),
        jnp.sum(jnp.where(earlier, rows_from_low(shear_rows)[None, :], 0), 1),
    )
    needed = reach[slices - 1]
    choice = sum((needed > 8 * size).astype(jnp.int32) for size in sizes[:-1])

    def with_groups(groups):
        early = (groups + 1) // 2
        late = groups - early

        def branch(volume, shear_rows, shear_cols, reach):
            middle = jnp.minimum(jnp.sum((reach <= 8 * early).astype(jnp.int32)), slices - 1)
            begin, end = jnp.zeros_like(middle), jnp.full_like(middle, slices)
            up_first, up_second, down_first, down_second = pack_halo(
                volume, shear_rows, early, late
            )
            high_first = lax.ppermute(up_first, "rows", backward)
            low_first = lax.ppermute(down_first, "rows", forward)
            if ORDERED:
                high_first, low_first, up_second, down_second = lax.optimization_barrier(
                    (high_first, low_first, up_second, down_second)
                )
            high_second = lax.ppermute(up_second, "rows", backward)
            low_second = lax.ppermute(down_second, "rows", forward)
            total = shear_part(
                "front", jnp.stack([begin, middle]), volume, shear_rows, shear_cols,
                (low_first, high_first), None, tiles,
            )
            return shear_part(
                "back", jnp.stack([middle, end]), volume, shear_rows, shear_cols,
                (low_first, low_second, high_first, high_second), total, tiles,
            )

        return branch

    image = lax.switch(
        choice, [with_groups(groups) for groups in sizes], volume, shear_rows, shear_cols, reach
    )
    pieces = lax.all_to_all(image, "depth", 0, 0, tiled=True)
    row_start = lax.axis_index("rows") * band_rows
    row_shifts = lax.dynamic_slice_in_dim(warp_cols, row_start, band_rows, 0)
    across, top, bottom = warp_columns(pieces, row_shifts[:, None], width)
    below = lax.ppermute(bottom, "rows", forward)
    above = lax.ppermute(top, "rows", backward)
    return warp_rows_of(across, below, above, warp_rows[None, :])


def solution(mesh):
    return jax.shard_map(
        per_device,
        mesh=mesh,
        in_specs=(P(None, "depth", "rows", None), P("depth"), P("depth"), P(), P("depth")),
        out_specs=P(None, "rows", "depth"),
        check_vma=False,
    )
```

time: 302 us -> 137 us (0.45); the launches traced: 306 us -> 134 us
  Pallas kernels: 147 us -> 58.6 us
  waiting for transfers between devices: 129 us -> 41.1 us
  starting transfers between devices: 27.2 us -> 22.8 us
  between operations: 0.05 us -> 3.3 us
    pallas_call x2 -> x3, Pallas kernels: 141 us -> 52 us  [the longest x2 45.9 us: shear_part(): pl.pallas_call(functools.partial(shear_kernel, part), out_shape=out, grid...]
    ppermute x2 -> x4, waiting for transfers between devices: 106 us -> 18.5 us  [the longest x1 12.8 us: branch(): low_first = lax.ppermute(down_first, 'rows', forward)]
    all_to_all x1, starting transfers between devices: 15.5 us -> 3.58 us  [per_device(): pieces = lax.all_to_all(image, 'depth', 0, 0, tiled=True)]
    ppermute x2 -> x4, starting transfers between devices: 5.83 us -> 13.4 us  [the longest x1 5.59 us: branch(): low_second = lax.ppermute(down_second, 'rows', forward)]
  transfers between devices with their start and end apart: 5 -> 7, of which waited for: 5 -> 5; matrix products, arithmetic and copies ran while one was open for 0% -> 2% of each run, Pallas kernels for 0% -> 15%
where the time goes in v3:
time: 137 us; the launch traced here: 134 us
  Pallas kernels  58.6 us (43%)
  waiting for transfers between devices  41.1 us (30%)
  starting transfers between devices  22.8 us (17%)
  local copies, waits for them, and re-layouts  4.96 us (4%)
  between operations  3.3 us (2%)
  other arithmetic  2.07 us (2%)
    pallas_call x2, Pallas kernels, shear_part(): pl.pallas_call(functools.partial(shear_kernel, part), out_shape=out, grid...  45.9 us
    all_to_all x1, waiting for transfers between devices, per_device(): pieces = lax.all_to_all(image, 'depth', 0, 0, tiled=True)  17.9 us
    ppermute x1, waiting for transfers between devices, branch(): low_first = lax.ppermute(down_first, 'rows', forward)  12.8 us
    pallas_call x1, Pallas kernels, pack_halo(): pl.pallas_call(pack_kernel, out_shape=(packed(early), packed(late), packe...  6.14 us
    ppermute x1, waiting for transfers between devices, branch(): high_first = lax.ppermute(up_first, 'rows', backward)  5.64 us
    ppermute x1, starting transfers between devices, branch(): low_second = lax.ppermute(down_second, 'rows', forward)  5.59 us
    ppermute x1, waiting for transfers between devices, per_device(): above = lax.ppermute(top, 'rows', backward)  4.03 us
    ppermute x1, starting transfers between devices, per_device(): above = lax.ppermute(top, 'rows', backward)  3.92 us
  transfers between devices with their start and end apart: 7, of which 5 were waited for; matrix products, arithmetic and copies ran while one was open for 2% of the time, Pallas kernels for 15%

profile of v3, /device:TPU:24, one launch (start us, length us, event | category | flops | bytes accessed | tf_op | source)
XLA Modules:
  0.0 133.8 jit_solution(3643735736990411745)
XLA Ops:
  0.0 0.7 subtract_maximum_fusion
  4.6 88.0 %conditional.1 = (bf16[8,4,32,640]{3,2,1,0:T(8,128)(2,1)}) conditional(s32[]{:T(128)} %bitcast.6, (s32[16]{0:T(128)S(1)}, s32[16]{0:T(128)}, bf16[4,16,32,4096]{3,2,1,0:T(8,128)(2,1)}, s32[16]{0:T(128)}) %tuple.23, (s32[16]{0:T(128)S(1)}, s32[16]{0:T(128)}, bf16[4,16,32,4096]{3,2,1,0:T(8,128)(2,1)}, ...), branch_computations={%region_2.4_spmd, %region_4.6_spmd, %region_6.8_spmd, %region_8.10... | conditional | flops 17179869184 | bytes 63964008 | solution.py:549
  4.7 6.1 %branch_1_fun.3 = (bf16[4,4,8,4096]{3,2,1,0:T(8,128)(2,1)}, bf16[3,4,8,4096]{3,2,1,0:T(8,128)(2,1)}, bf16[4,4,8,4096]{3,2,1,0:T(8,128)(2,1)}, bf16[3,4,8,4096]{3,2,1,0:T(8,128)(2,1)}) custom-call(s32[16]{0:T(128)} %get-tuple-element.68.shear_rows.refs_0_, bf16[4,16,32,4096]{3,2,1,0:T(8,128)(2,1)} %get-tuple-element.71.volume_ref.refs_3_), custom_call_target="tpu_custom_call" | custom-call | tf_op jit(solution)/shard_map/cond/branch_1_fun/pallas_call | solution.py:152
  10.8 3.5 %collective-permute-start.4 = (bf16[4,4,8,4096]{3,2,1,0:T(8,128)(2,1)}, bf16[4,4,8,4096]{3,2,1,0:T(8,128)(2,1)S(1)}, u32[]{:S(2)}, u32[]{:S(2)}) collective-permute-start(bf16[4,4,8,4096]{3,2,1,0:T(8,128)(2,1)} %get-tuple-element.72), channel_id=1, source_target_pairs={{0,1},{1,2},{2,3},{3,4},{4,5},{5,6},{6,7},{7,8},{8,9},{9,10},{10,1... | collective-permute-start | bytes 3145736 | tf_op jit(solution)/shard_map/cond/branch_1_fun/ppermute | solution.py:531
  14.3 2.4 %collective-permute-start.6 = (bf16[4,4,8,4096]{3,2,1,0:T(8,128)(2,1)}, bf16[4,4,8,4096]{3,2,1,0:T(8,128)(2,1)S(1)}, u32[]{:S(2)}, u32[]{:S(2)}) collective-permute-start(bf16[4,4,8,4096]{3,2,1,0:T(8,128)(2,1)} %get-tuple-element.74), channel_id=1, source_target_pairs={{1,0},{2,1},{3,2},{4,3},{5,4},{6,5},{7,6},{8,7},{9,8},{10,9},{11,1... | collective-permute-start | bytes 3145736 | tf_op jit(solution)/shard_map/cond/branch_1_fun/ppermute | solution.py:530
  16.7 5.6 %collective-permute-start.5 = (bf16[3,4,8,4096]{3,2,1,0:T(8,128)(2,1)}, bf16[3,4,8,4096]{3,2,1,0:T(8,128)(2,1)S(1)}, u32[]{:S(2)}, u32[]{:S(2)}) collective-permute-start(bf16[3,4,8,4096]{3,2,1,0:T(8,128)(2,1)} %get-tuple-element.73), channel_id=1, source_target_pairs={{0,1},{1,2},{2,3},{3,4},{4,5},{5,6},{6,7},{7,8},{8,9},{9,10},{10,1... | collective-permute-start | bytes 2359304 | tf_op jit(solution)/shard_map/cond/branch_1_fun/ppermute | solution.py:537
  22.3 1.9 %collective-permute-start.7 = (bf16[3,4,8,4096]{3,2,1,0:T(8,128)(2,1)}, bf16[3,4,8,4096]{3,2,1,0:T(8,128)(2,1)}, u32[]{:S(2)}, u32[]{:S(2)}) collective-permute-start(bf16[3,4,8,4096]{3,2,1,0:T(8,128)(2,1)} %get-tuple-element.75), channel_id=1, source_target_pairs={{1,0},{2,1},{3,2},{4,3},{5,4},{6,5},{7,6},{8,7},{9,8},{10,9},{11,1... | collective-permute-start | bytes 2359304 | tf_op jit(solution)/shard_map/cond/branch_1_fun/ppermute | solution.py:536
  24.2 0.7 fusion.1
  26.1 12.8 %collective-permute-done.4.refs_4_ = bf16[4,4,8,4096]{3,2,1,0:T(8,128)(2,1)S(1)} collective-permute-done((bf16[4,4,8,4096]{3,2,1,0:T(8,128)(2,1)}, bf16[4,4,8,4096]{3,2,1,0:T(8,128)(2,1)S(1)}, u32[]{:S(2)}, u32[]{:S(2)}) %collective-permute-start.4) | collective-permute-done | bytes 1048608 | tf_op jit(solution)/shard_map/cond/branch_1_fun/ppermute | solution.py:531
  39.0 5.6 %collective-permute-done.6.refs_5_.refs_6_ = bf16[4,4,8,4096]{3,2,1,0:T(8,128)(2,1)S(1)} collective-permute-done((bf16[4,4,8,4096]{3,2,1,0:T(8,128)(2,1)}, bf16[4,4,8,4096]{3,2,1,0:T(8,128)(2,1)S(1)}, u32[]{:S(2)}, u32[]{:S(2)}) %collective-permute-start.6) | collective-permute-done | bytes 1048608 | tf_op jit(solution)/shard_map/cond/branch_1_fun/ppermute | solution.py:530
  44.6 1.0 copy-done.17
  45.6 20.2 %branch_1_fun.4.refs_8_ = f32[4,32,4096]{2,1,0:T(8,128)} custom-call(s32[16]{0:T(128)S(1)} %copy-done.5, s32[16]{0:T(128)S(1)} %copy-done.26, s32[2]{0:T(128)} %get-tuple-element.117.refs_2_, bf16[4,16,32,4096]{3,2,1,0:T(8,128)(2,1)} %get-tuple-element.71.volume_ref.refs_3_, bf16[4,4,8,4096]{3,2,1,0:T(8,128)(2,1)} %copy-done.15, ...), custom_call_target="tpu_custom_call" | custom-call | flops 8589934592 | bytes 8388608 | tf_op jit(solution)/shard_map/cond/branch_1_fun/pallas_call | solution.py:400
  65.8 0.9 copy-done.23
  66.7 25.7 %branch_1_fun.5 = bf16[8,4,32,640]{3,2,1,0:T(8,128)(2,1)} custom-call(s32[16]{0:T(128)S(1)} %copy-done.5, s32[16]{0:T(128)S(1)} %copy-done.26, s32[2]{0:T(128)} %get-tuple-element.116.refs_2_, bf16[4,16,32,4096]{3,2,1,0:T(8,128)(2,1)} %get-tuple-element.71.volume_ref.refs_3_, bf16[4,4,8,4096]{3,2,1,0:T(8,128)(2,1)} %copy-done.15, ...), custom_call_target="tpu_custom_call" | custom-call | flops 8589934592 | bytes 8388608 | tf_op jit(solution)/shard_map/cond/branch_1_fun/pallas_call | solution.py:400
  92.7 3.6 %all-to-all-start = ((bf16[8,4,32,640]{3,2,1,0:T(8,128)(2,1)}), bf16[8,4,32,640]{3,2,1,0:T(8,128)(2,1)S(1)}, u32[]{:S(2)}, u32[]{:S(2)}) async-start(bf16[8,4,32,640]{3,2,1,0:T(8,128)(2,1)} %get-tuple-element.130), calls=%async_computation | async-start | bytes 2621440 | tf_op jit(solution)/shard_map/all_to_all | solution.py:552
  96.4 0.7 copy.7.shifts_ref
  97.0 17.9 %all-to-all-done.pieces_ref = bf16[8,4,32,640]{3,2,1,0:T(8,128)(2,1)S(1)} async-done(((bf16[8,4,32,640]{3,2,1,0:T(8,128)(2,1)}), bf16[8,4,32,640]{3,2,1,0:T(8,128)(2,1)S(1)}, u32[]{:S(2)}, u32[]{:S(2)}) %all-to-all-start) | async-done | bytes 1310752 | tf_op jit(solution)/shard_map/all_to_all | solution.py:552
  115.0 1.1 copy-done.1
  116.1 3.7 %shard_map.55 = (f32[4,32,512]{2,1,0:T(8,128)}, f32[36,512]{1,0:T(8,128)}, f32[36,512]{1,0:T(8,128)}) custom-call(bf16[8,4,32,640]{3,2,1,0:T(8,128)(2,1)} %copy-done.1, s32[32,1]{1,0:T(8,128)} %copy.7.shifts_ref), custom_call_target="tpu_custom_call" | custom-call | tf_op jit(solution)/shard_map/pallas_call | solution.py:458
  119.8 1.9 %collective-permute-start.24 = (f32[36,512]{1,0:T(8,128)}, f32[36,512]{1,0:T(8,128)S(1)}, u32[]{:S(2)}, u32[]{:S(2)}) collective-permute-start(f32[36,512]{1,0:T(8,128)} %get-tuple-element.112), channel_id=1, source_target_pairs={{0,1},{1,2},{2,3},{3,4},{4,5},{5,6},{6,7},{7,8},{8,9},{9,10},{10,1... | collective-permute-start | bytes 221192 | tf_op jit(solution)/shard_map/ppermute | solution.py:556
  121.7 3.9 %collective-permute-start.25 = (f32[36,512]{1,0:T(8,128)}, f32[36,512]{1,0:T(8,128)S(1)}, u32[]{:S(2)}, u32[]{:S(2)}) collective-permute-start(f32[36,512]{1,0:T(8,128)} %get-tuple-element.113), channel_id=1, source_target_pairs={{1,0},{2,1},{3,2},{4,3},{5,4},{6,5},{7,6},{8,7},{9,8},{10,9},{11,1... | collective-permute-start | bytes 221192 | tf_op jit(solution)/shard_map/ppermute | solution.py:557
  125.6 0.7 collective-permute-done.24.low_ref
  126.3 4.0 %collective-permute-done.25.high_ref = f32[36,512]{1,0:T(8,128)S(1)} collective-permute-done((f32[36,512]{1,0:T(8,128)}, f32[36,512]{1,0:T(8,128)S(1)}, u32[]{:S(2)}, u32[]{:S(2)}) %collective-permute-start.25) | collective-permute-done | bytes 73760 | tf_op jit(solution)/shard_map/ppermute | solution.py:557
  131.0 2.8 %shard_map.56 = f32[4,32,512]{2,1,0:T(8,128)} custom-call(f32[4,32,512]{2,1,0:T(8,128)} %get-tuple-element.111.across_ref, f32[36,512]{1,0:T(8,128)} %copy-done.2, f32[36,512]{1,0:T(8,128)} %copy-done.3, s32[1,512]{1,0:T(1,128)} %bitcast.10), custom_call_target="tpu_custom_call" | custom-call | tf_op jit(solution)/shard_map/pallas_call | solution.py:489
  (22 shorter events, 2.1 us)
Async XLA Ops:
  0.0 96.3 %copy-start = (s32[512]{0:T(512)S(1)}, s32[512]{0:T(512)}, u32[]{:S(2)}) copy-start(s32[512]{0:T(512)} %param.14) | copy-start | bytes 6148
  4.7 40.9 %copy-start.5 = (s32[16]{0:T(128)S(1)}, s32[16]{0:T(128)}, u32[]{:S(2)}) copy-start(s32[16]{0:T(128)} %get-tuple-element.68.shear_rows.refs_0_) | copy-start | bytes 196 | tf_op jit(solution)/shard_map/cond
  4.7 40.9 %copy-start.26 = (s32[16]{0:T(128)S(1)}, s32[16]{0:T(128)}, u32[]{:S(2)}) copy-start(s32[16]{0:T(128)} %get-tuple-element.69.refs_1_) | copy-start | bytes 196 | tf_op jit(solution)/shard_map/cond
  10.8 28.2 %collective-permute-start.4 = (bf16[4,4,8,4096]{3,2,1,0:T(8,128)(2,1)}, bf16[4,4,8,4096]{3,2,1,0:T(8,128)(2,1)S(1)}, u32[]{:S(2)}, u32[]{:S(2)}) collective-permute-start(bf16[4,4,8,4096]{3,2,1,0:T(8,128)(2,1)} %get-tuple-element.72), channel_id=1, source_target_pairs={{0,1},{1,2},{2,3},{3,4},{4,5},{5,6},{6,7},{7,8},{8,9},{9,10},{10,1... | collective-permute-start | bytes 3145736 | tf_op jit(solution)/shard_map/cond/branch_1_fun/ppermute | solution.py:531
  14.3 30.3 %collective-permute-start.6 = (bf16[4,4,8,4096]{3,2,1,0:T(8,128)(2,1)}, bf16[4,4,8,4096]{3,2,1,0:T(8,128)(2,1)S(1)}, u32[]{:S(2)}, u32[]{:S(2)}) collective-permute-start(bf16[4,4,8,4096]{3,2,1,0:T(8,128)(2,1)} %get-tuple-element.74), channel_id=1, source_target_pairs={{1,0},{2,1},{3,2},{4,3},{5,4},{6,5},{7,6},{8,7},{9,8},{10,9},{11,1... | collective-permute-start | bytes 3145736 | tf_op jit(solution)/shard_map/cond/branch_1_fun/ppermute | solution.py:530
  16.7 49.1 %collective-permute-start.5 = (bf16[3,4,8,4096]{3,2,1,0:T(8,128)(2,1)}, bf16[3,4,8,4096]{3,2,1,0:T(8,128)(2,1)S(1)}, u32[]{:S(2)}, u32[]{:S(2)}) collective-permute-start(bf16[3,4,8,4096]{3,2,1,0:T(8,128)(2,1)} %get-tuple-element.73), channel_id=1, source_target_pairs={{0,1},{1,2},{2,3},{3,4},{4,5},{5,6},{6,7},{7,8},{8,9},{9,10},{10,1... | collective-permute-start | bytes 2359304 | tf_op jit(solution)/shard_map/cond/branch_1_fun/ppermute | solution.py:537
  22.3 43.5 %collective-permute-start.7 = (bf16[3,4,8,4096]{3,2,1,0:T(8,128)(2,1)}, bf16[3,4,8,4096]{3,2,1,0:T(8,128)(2,1)}, u32[]{:S(2)}, u32[]{:S(2)}) collective-permute-start(bf16[3,4,8,4096]{3,2,1,0:T(8,128)(2,1)} %get-tuple-element.75), channel_id=1, source_target_pairs={{1,0},{2,1},{3,2},{4,3},{5,4},{6,5},{7,6},{8,7},{9,8},{10,9},{11,1... | collective-permute-start | bytes 2359304 | tf_op jit(solution)/shard_map/cond/branch_1_fun/ppermute | solution.py:536
  39.0 5.6 %copy-start.15 = (bf16[4,4,8,4096]{3,2,1,0:T(8,128)(2,1)}, bf16[4,4,8,4096]{3,2,1,0:T(8,128)(2,1)S(1)}, u32[]{:S(2)}) copy-start(bf16[4,4,8,4096]{3,2,1,0:T(8,128)(2,1)S(1)} %collective-permute-done.4.refs_4_) | copy-start | bytes 3145732 | tf_op jit(solution)/shard_map/cond
  44.6 1.0 copy-start.17
  65.8 0.9 copy-start.23
  92.7 22.3 %all-to-all-start = ((bf16[8,4,32,640]{3,2,1,0:T(8,128)(2,1)}), bf16[8,4,32,640]{3,2,1,0:T(8,128)(2,1)S(1)}, u32[]{:S(2)}, u32[]{:S(2)}) async-start(bf16[8,4,32,640]{3,2,1,0:T(8,128)(2,1)} %get-tuple-element.130), calls=%async_computation | async-start | bytes 2621440 | tf_op jit(solution)/shard_map/all_to_all | solution.py:552
  115.0 1.1 copy-start.1
  119.8 6.5 %collective-permute-start.24 = (f32[36,512]{1,0:T(8,128)}, f32[36,512]{1,0:T(8,128)S(1)}, u32[]{:S(2)}, u32[]{:S(2)}) collective-permute-start(f32[36,512]{1,0:T(8,128)} %get-tuple-element.112), channel_id=1, source_target_pairs={{0,1},{1,2},{2,3},{3,4},{4,5},{5,6},{6,7},{7,8},{8,9},{9,10},{10,1... | collective-permute-start | bytes 221192 | tf_op jit(solution)/shard_map/ppermute | solution.py:556
  121.7 8.7 %collective-permute-start.25 = (f32[36,512]{1,0:T(8,128)}, f32[36,512]{1,0:T(8,128)S(1)}, u32[]{:S(2)}, u32[]{:S(2)}) collective-permute-start(f32[36,512]{1,0:T(8,128)} %get-tuple-element.113), channel_id=1, source_target_pairs={{1,0},{2,1},{3,2},{4,3},{5,4},{6,5},{7,6},{8,7},{9,8},{10,9},{11,1... | collective-permute-start | bytes 221192 | tf_op jit(solution)/shard_map/ppermute | solution.py:557
  126.3 4.0 %copy-start.2 = (f32[36,512]{1,0:T(8,128)}, f32[36,512]{1,0:T(8,128)S(1)}, u32[]{:S(2)}) copy-start(f32[36,512]{1,0:T(8,128)S(1)} %collective-permute-done.24.low_ref) | copy-start | bytes 221188
  130.4 0.6 copy-start.3
